TPU v7x, 32 devices: a whole 2x2x4 slice. The times are simulated.
32 devices in a mesh: band: 4 (over y, x), pair: 8 (over z, core).
Axes of the slice: x: 2, y: 2, z: 4, core: 2. Of those that a mesh axis runs over, the one named last changes fastest.
Arguments:
- visibilities: float32 [4, 16, 8, 2, 1024], P('band', 'pair'), may hold values from -6 to 6
- coherencies: bfloat16 [4, 16, 8, 2, 32, 1024], P('band', 'pair'), may hold values from -1 to 1
- block_tiles: int32 [16, 2], P('pair'), may hold values from 0 to 15, as said below
- sample_counts: int32 [16], P('pair'), may hold values from 1 to 8, as said below
- gains: float32 [4, 2, 32, 512], P('band', None, None, 'pair'), may hold values from 0.5 to 1.5
- targets: float32 [4, 2, 32, 512], P('band', None, None, 'pair'), may hold values from 0.5 to 1.5
- multipliers: float32 [4, 2, 32, 512], P('band', None, None, 'pair'), may hold values from -2 to 2
Outputs:
- new_gains: float32 [4, 2, 32, 512], P('band', None, None, 'pair')
- new_targets: float32 [4, 2, 32, 512], P('band', None, None, 'pair')
- new_multipliers: float32 [4, 2, 32, 512], P('band', None, None, 'pair')
Inputs may be any that keep to these rules, and one draw needn't show every extreme that they name: `block_tiles`: each row names two station tiles a <= b; no tile pair appears twice; the pairs (0, 15) and (15, 15) are always among them. `sample_counts`: some block has all 8 samples and some block only one.
All inputs are finite; a program needn't handle non-finite values.
Results may differ from a plain program's by a relative error of at most 0.0003.
Values sent between devices are 32-bit elements; how exact they have to be, the bound alone decides.
No kernel may reach another device: no remote copies, remote signals or barrier semaphores. Data moves between devices by JAX's collectives and lax.ppermute only.
A program may use at most 64 MiB of HBM per device.

v0:
```python
import math

import jax
import jax.numpy as jnp
import numpy as np
from jax import lax
from jax.experimental import pallas as pl
from jax.experimental.pallas import tpu as pltpu
from jax.sharding import PartitionSpec as P


P_SIZE = 8
TILE = 32
LANES = 128
HALF = LANES // 2
GROUP = LANES // TILE
PIECES = 2

ridge = 0.05
penalty = 0.25


def fit_matrix(freq_count, term_count):
    positions = (np.arange(freq_count) + 0.5) / freq_count
    basis = np.stack(
        [
            math.comb(term_count - 1, degree)
            * positions**degree
            * (1.0 - positions) ** (term_count - 1 - degree)
            for degree in range(term_count)
        ],
        axis=1,
    )
    normal = basis.T @ basis + ridge * np.eye(term_count)
    factor = np.linalg.cholesky(normal)
    half = np.linalg.solve(factor, basis.T)
    return half.T @ half


class Plan:
    def __init__(self, directions, stations, pairs, blocks, times, cells):
        self.k = directions
        self.sl = stations
        self.zn = pairs // 2
        self.blocks = blocks
        self.times = times
        self.cells = cells
        self.steps = cells // LANES
        self.total = blocks * self.steps
        self.per = stations // TILE
        self.parts = 1 if self.per else TILE // stations
        self.rows = 2 * directions + 8 * ((blocks + 7) // 8)
        assert 2 * stations <= LANES and directions == 32 and times <= 8 and self.steps == 8

    def lane(self, rows=None):
        return lax.broadcasted_iota(jnp.int32, (self.k if rows is None else rows, LANES), 1)

    def owner(self, me, device):
        return (device % 2) == (me % 2), (device // 2) ^ (me // 2)

    def record(self, me, own_ref, sib_ref, device, row):
        same, slot = self.owner(me, device)
        own = own_ref[slot, row : row + self.k, :]
        sib = sib_ref[slot, row : row + self.k, :]
        return jnp.where(same, own, sib)

    def fetch(self, me, own_ref, sib_ref, tile, row):
        lane = self.lane()
        part, spot = lane // HALF, lane % TILE
        if self.sl == HALF:
            device = lax.shift_right_logical(tile, 1)
            sub = lax.bitwise_and(tile, 1)
            rec = self.record(me, own_ref, sib_ref, device, row)
            return jnp.where(sub == 1, pltpu.roll(rec, LANES - TILE, 1), rec)
        if self.per:
            device = tile // self.per
            sub = tile - device * self.per
            rec = self.record(me, own_ref, sib_ref, device, row)
            return take(rec, part * self.sl + sub * TILE + spot)
        value = None
        for r in range(self.parts):
            rec = self.record(me, own_ref, sib_ref, tile * self.parts + r, row)
            here = take(rec, part * self.sl + spot % self.sl)
            value = here if value is None else jnp.where(spot // self.sl == r, here, value)
        return value

    def place(self, terms, side, sub):
        lane = self.lane()
        if self.sl == HALF:
            moved = pltpu.roll(terms, TILE if side == 0 else LANES - TILE, 1)
            return jnp.where(lane // TILE % 2 == sub, jnp.where(sub == side, terms, moved), 0.0)
        part, spot = lane // self.sl % 2, lane % self.sl
        start = part * HALF + side * TILE
        if self.per:
            value = take(terms, start + spot % TILE)
            keep = spot // TILE == sub
        else:
            value = take(terms, start + sub * self.sl + spot)
            keep = lane < 2 * self.sl
        return jnp.where(keep, value, 0.0)

    def spread(self, me, tile, terms, side, own_ref, sib_ref):
        if self.per:
            device = tile // self.per
            spots = [(device, tile - device * self.per)]
        else:
            spots = [(tile * self.parts + r, r) for r in range(self.parts)]
        for device, sub in spots:
            value = self.place(terms, side, sub)
            same, slot = self.owner(me, device)
            own_ref[slot] = own_ref[slot] + jnp.where(same, value, 0.0)
            sib_ref[slot] = sib_ref[slot] + jnp.where(same, 0.0, value)

    def record_of(self, raw_ref):
        pieces = [raw_ref[0, 0], raw_ref[0, 1]]
        if 2 * self.sl < LANES:
            pieces.append(jnp.zeros((self.k, LANES - 2 * self.sl), jnp.float32))
        return jnp.concatenate(pieces, axis=1)


def take(value, lanes):
    return jnp.take_along_axis(value, lanes, axis=1, mode="promise_in_bounds")


def pieces(value, count):
    result = []
    for _ in range(count):
        result.append(value.astype(jnp.bfloat16))
        value = value - result[-1].astype(jnp.float32)
    return result


def matmul(lhs, rhs):
    return jnp.dot(lhs, rhs, preferred_element_type=jnp.float32)


def eights(value):
    return [value[8 * i : 8 * i + 8] for i in range(value.shape[0] // 8)]


def pack_kernel(plan, tiles_hbm, counts_hbm, gains_hbm, targets_hbm, mult_hbm, out_ref, meta_ref, bound_ref, mrec_ref, *scratch):
    bufs, sems = scratch[:-1], scratch[-1]
    copies = [
        pltpu.make_async_copy(src, dst, sems.at[i])
        for i, (src, dst) in enumerate(zip((gains_hbm, targets_hbm, mult_hbm, tiles_hbm, counts_hbm), bufs))
    ]
    for copy in copies:
        copy.start()
    for copy in copies:
        copy.wait()
    gains_ref, targets_ref, mult_ref, tiles_ref, counts_ref = bufs
    k = plan.k
    gain = plan.record_of(gains_ref)
    target = plan.record_of(targets_ref)
    mult = plan.record_of(mult_ref)
    out_ref[:k] = gain
    out_ref[k : 2 * k] = gain - penalty * (gain - target + mult)
    mrec_ref[...] = mult
    lane = plan.lane(8)
    sub = lax.broadcasted_iota(jnp.int32, (8, LANES), 0)
    tiles = tiles_ref[...]
    counts = counts_ref[...]
    meta = jnp.zeros((8, LANES), jnp.int32)
    for base in range(0, plan.blocks, 8):
        rows = jnp.zeros((8, LANES), jnp.int32)
        for n in range(base, min(base + 8, plan.blocks)):
            one, two, count = tiles[n, 0], tiles[n, 1], counts[0, n]
            ids = jnp.where(lane // TILE % 2 == 0, one, two)
            rows = jnp.where(sub == n - base, ids, rows)
            meta = jnp.where(lane == 2 * n, one, jnp.where(lane == 2 * n + 1, two, meta))
            bound_ref[n, 0] = jnp.full((8, LANES), count, jnp.int32)
            bound_ref[n, 1] = jnp.full((8, LANES), jnp.where(one != two, plan.cells, 0), jnp.int32)
        out_ref[2 * k + base : 2 * k + base + 8] = rows.astype(jnp.float32)
    meta_ref[...] = meta


def load_kernel(plan, vis_hbm, coh_hbm, vis_ref, coh_ref, vis_buf, coh_buf, sems):
    chunks = 4
    per = plan.steps // chunks
    copies = []
    for n in range(plan.blocks):
        for c in range(chunks):
            lanes = pl.ds(c * per * LANES, per * LANES)
            copies.append(
                pltpu.make_async_copy(
                    coh_hbm.at[0, n, :, :, :, lanes],
                    coh_buf.at[n, :, :, :, lanes],
                    sems.at[n * chunks + c],
                )
            )
    last = pltpu.make_async_copy(vis_hbm.at[0], vis_buf, sems.at[plan.blocks * chunks])
    for copy in copies:
        copy.start()
    last.start()
    for n in range(plan.blocks):
        for c in range(chunks):
            copies[n * chunks + c].wait()

            def convert(t, carry, n=n, c=c):
                for index in range(c * per, (c + 1) * per):
                    lanes = pl.ds(index * LANES, LANES)
                    real = coh_buf[n, t, 0, :, lanes].astype(jnp.float32)
                    imag = coh_buf[n, t, 1, :, lanes].astype(jnp.float32)
                    q = n * plan.steps + index
                    coh_ref[q, t, 0] = real
                    coh_ref[q, t, 1] = real + imag
                    coh_ref[q, t, 2] = real - imag
                return carry

            lax.fori_loop(0, plan.times, convert, 0)
    last.wait()
    for n in range(plan.blocks):
        for part in range(2):
            value = vis_buf[n, :, part, :]
            for index in range(plan.steps):
                vis_ref[n * plan.steps + index, part] = value[:, index * LANES : (index + 1) * LANES]


def table_kernel(plan, spread_ref, narrow_ref, fold_ref):
    record = lax.broadcasted_iota(jnp.int32, (LANES, LANES), 0)
    cell = lax.broadcasted_iota(jnp.int32, (LANES, LANES), 1)
    spread = cell // TILE - record
    narrow = record // TILE - cell
    fold = TILE + record % TILE - cell
    for part in range(2):
        for index in range(plan.steps):
            span = slice((2 * index + part) * LANES, (2 * index + part + 1) * LANES)
            offset = -(part * HALF + index * GROUP)
            spread_ref[:, span] = jnp.where(spread == offset, 1.0, 0.0).astype(jnp.bfloat16)
            narrow_ref[span, :] = jnp.where(narrow == offset, 1.0, 0.0).astype(jnp.bfloat16)
        hit = jnp.where(fold == -part * HALF, 1.0, 0.0).astype(jnp.bfloat16)
        fold_ref[part * LANES : (part + 1) * LANES, :] = hit


def block_gradients(
    plan, bound_ref, tile_gains, vis_ref, coh_ref, spread_ref, narrow_ref, fold_ref,
    right_ref, wide_ref, second_ref, first_ref, model_ref, error_ref,
):
    k, times, steps = plan.k, plan.times, plan.steps
    shift = steps.bit_length() - 1
    lane_k = plan.lane()
    lane = plan.lane(8)
    sample = lax.broadcasted_iota(jnp.int32, (8, LANES), 0)
    lefts = [piece for left, _ in tile_gains for piece in pieces(left, 3)]
    lefts = matmul(jnp.concatenate(lefts, axis=0), spread_ref[...])
    for n in range(plan.blocks):
        rows = [lefts[(3 * n + i) * k : (3 * n + i + 1) * k] for i in range(3)]
        value = rows[0] + rows[1] + rows[2]
        for index in range(steps):
            for part in range(2):
                start = (2 * index + part) * LANES
                wide_ref[n * steps + index, part] = value[:, start : start + LANES]
    for n, (left, right) in enumerate(tile_gains):
        pairs = jnp.where(lane_k // TILE % 2 == 0, right, pltpu.roll(right, TILE, 1))
        other = pltpu.roll(pairs, HALF, 1)
        right_ref[n, 0] = jnp.where(lane_k < HALF, pairs, other)
        right_ref[n, 1] = jnp.where(lane_k < HALF, other, pairs)
        second_ref[n] = jnp.zeros((2, k, LANES), jnp.float32)

    def where_is(q):
        q = jnp.int32(q)
        return lax.shift_right_logical(q, shift), lax.bitwise_and(q, steps - 1)

    def residual(q):
        n, index = where_is(q)
        lr, li = wide_ref[q, 0], wide_ref[q, 1]
        rr, ri = right_ref[n, 0], right_ref[n, 1]
        pr = lr * rr + li * ri
        pi = li * rr - lr * ri
        ps = pr + pi
        for t in range(times):
            both = sum(eights(ps * coh_ref[q, t, 0]))
            model_ref[0, 8 * t : 8 * t + 8] = both - sum(eights(pi * coh_ref[q, t, 1]))
            model_ref[1, 8 * t : 8 * t + 8] = both - sum(eights(pr * coh_ref[q, t, 2]))
        mr, mi = (sum(model_ref[part, pl.ds(j, times, stride=8), :] for j in range(8)) for part in range(2))
        upper = index * GROUP + lane // TILE - lane % TILE
        keep = ((upper < bound_ref[n, 1]) & (sample < bound_ref[n, 0]))[:times]
        er = jnp.where(keep, vis_ref[q, 0] - mr, 0.0)
        ei = jnp.where(keep, vis_ref[q, 1] - mi, 0.0)
        slot = lax.bitwise_and(jnp.int32(q), 1)
        error_ref[slot, 0, :times] = er + ei
        error_ref[slot, 1, :times] = ei
        error_ref[slot, 2, :times] = er

    def gradient(q):
        n, index = where_is(q)
        slot = lax.bitwise_and(jnp.int32(q), 1)
        sums = [None] * 3
        for t in range(times):
            for j, c in enumerate((0, 2, 1)):
                e = error_ref[slot, j, pl.ds(t, 8, stride=0), :]
                value = [e * part for part in eights(coh_ref[q, t, c])]
                sums[j] = value if t == 0 else [x + y for x, y in zip(sums[j], value)]
        both, lone_re, lone_im = (jnp.concatenate(value, axis=0) for value in sums)
        acc_re = both - lone_re
        acc_im = both - lone_im
        lr, li = wide_ref[q, 0], wide_ref[q, 1]
        rr, ri = right_ref[n, 0], right_ref[n, 1]
        second_ref[n, 0] = second_ref[n, 0] + (acc_re * lr + acc_im * li)
        second_ref[n, 1] = second_ref[n, 1] + (acc_re * li - acc_im * lr)
        terms = jnp.concatenate([acc_re * rr - acc_im * ri, acc_re * ri + acc_im * rr], axis=1)
        lanes = pl.ds(pl.multiple_of(index * 2 * LANES, 2 * LANES), 2 * LANES)
        for i, piece in enumerate(pieces(terms, PIECES)):
            rows = pl.ds(pl.multiple_of((n * PIECES + i) * k, k), k)
            first_ref[rows, lanes] = piece

    final = plan.total - 1

    def step(q, carry):
        gradient(q)
        residual(q + 1)
        return carry

    residual(0)
    lax.fori_loop(0, final, step, 0, unroll=5)
    gradient(final)

    parts = []
    for n in range(plan.blocks):
        parts += pieces(jnp.concatenate([second_ref[n, 0], second_ref[n, 1]], axis=1), PIECES)
    value = matmul(jnp.concatenate(parts, axis=0), fold_ref[...])
    value = value + matmul(first_ref[...], narrow_ref[...])
    return [
        sum(value[(n * PIECES + i) * k : (n * PIECES + i + 1) * k] for i in range(PIECES))
        for n in range(plan.blocks)
    ]


def tile_ids(plan, meta_ref):
    meta = meta_ref[0:1, :]
    return [meta[0, i] for i in range(2 * plan.blocks)]


def first_kernel(plan, meta_ref, bound_ref, own_ref, sib_ref, vis_ref, coh_ref, spread_ref, narrow_ref, fold_ref, out_ref, *scratch):
    fixed = (vis_ref, coh_ref, spread_ref, narrow_ref, fold_ref)
    me = lax.axis_index("pair")
    records = [plan.fetch(me, own_ref, sib_ref, tile, 0) for tile in tile_ids(plan, meta_ref)]
    tile_gains = [records[2 * n : 2 * n + 2] for n in range(plan.blocks)]
    for n, terms in enumerate(block_gradients(plan, bound_ref, tile_gains, *fixed, *scratch)):
        out_ref[n] = terms


def gather_terms(plan, pay_ref, term_ref, tiles):
    k = plan.k
    labels = [tile.astype(jnp.float32) for tile in tiles]

    def add(slot, sums):
        ids_all = pay_ref[slot, 2 * k : plan.rows, :]
        for n in range(plan.blocks):
            ids = ids_all[n : n + 1]
            terms = term_ref[slot, n]
            sums = [s + jnp.where(ids == label, terms, 0.0) for s, label in zip(sums, labels)]
        return sums

    sums = [jnp.zeros((k, LANES), jnp.float32) for _ in labels]
    if plan.zn <= 4:
        for slot in range(plan.zn):
            sums = add(slot, sums)
    else:
        sums = lax.fori_loop(0, plan.zn, add, sums)
    return [s + pltpu.roll(s, LANES - TILE, 1) for s in sums]


def own_tiles(plan, me):
    if plan.per:
        return [me * plan.per + s for s in range(plan.per)]
    return [me // plan.parts]


def near_kernel(plan, step_size, meta_ref, own_ref, sib_ref, term_ref, records_ref, mine_ref):
    me = lax.axis_index("pair")
    tiles = tile_ids(plan, meta_ref)
    for i, value in enumerate(gather_terms(plan, own_ref, term_ref, tiles)):
        records_ref[i] = plan.fetch(me, own_ref, sib_ref, tiles[i], plan.k) + step_size * value
    for i, value in enumerate(gather_terms(plan, own_ref, term_ref, own_tiles(plan, me))):
        mine_ref[i] = value


def rest_kernel(plan, step_size, own_ref, sib_ref, term_ref, mine_ref, mult_ref, rest_ref):
    k = plan.k
    me = lax.axis_index("pair")
    sums = gather_terms(plan, sib_ref, term_ref, own_tiles(plan, me))
    mine = [mine_ref[i] + value for i, value in enumerate(sums)]
    if plan.per:
        own_sum = sum(plan.place(value, 0, s) for s, value in enumerate(mine))
    else:
        own_sum = plan.place(mine[0], 0, me % plan.parts)
    start = own_ref[0, :k, :]
    base = own_ref[0, k : 2 * k, :]
    pull = base - (1.0 - penalty) * start
    rest = (1.0 - penalty) * (base + step_size * own_sum) + pull
    rest_ref[0] = rest
    rest_ref[1] = rest + mult_ref[...]


def second_kernel(
    plan, step_size, meta_ref, bound_ref, sib_ref, term_ref, records_ref,
    vis_ref, coh_ref, spread_ref, narrow_ref, fold_ref, part_own_ref, part_sib_ref, *scratch,
):
    fixed = (vis_ref, coh_ref, spread_ref, narrow_ref, fold_ref)
    me = lax.axis_index("pair")
    tiles = tile_ids(plan, meta_ref)
    sums = gather_terms(plan, sib_ref, term_ref, tiles)
    records = [records_ref[i] + step_size * value for i, value in enumerate(sums)]
    tile_gains = [records[2 * n : 2 * n + 2] for n in range(plan.blocks)]
    part_own_ref[...] = jnp.zeros_like(part_own_ref)
    part_sib_ref[...] = jnp.zeros_like(part_sib_ref)
    for n, terms in enumerate(block_gradients(plan, bound_ref, tile_gains, *fixed, *scratch)):
        for side in range(2):
            plan.spread(me, tiles[2 * n + side], terms, side, part_own_ref, part_sib_ref)


def fit_kernel(plan, fit, gain_ref, own_ref, *refs):
    others, (gain_out, target_out, mult_out) = refs[:-3], refs[-3:]
    sl = plan.sl
    band = lax.axis_index("band")
    total = None
    for m, ref in enumerate((own_ref,) + tuple(others)):
        factor = jnp.float32(0.0)
        for f in range(fit.shape[0]):
            factor = jnp.where(band == f, jnp.float32(fit[f, f ^ m]), factor)
        value = factor * ref[...]
        total = value if total is None else total + value
    change = own_ref[...] - total
    gain = gain_ref[...]
    for part in range(2):
        lanes = slice(part * sl, (part + 1) * sl)
        gain_out[0, part] = gain[:, lanes]
        target_out[0, part] = total[:, lanes]
        mult_out[0, part] = change[:, lanes]


def exchange(value, axis, size, mask):
    return lax.ppermute(value, axis, [(i, i ^ mask) for i in range(size)])


def local(visibilities, coherencies, block_tiles, sample_counts, gains, targets, multipliers):
    pairs = lax.axis_size("pair")
    bands = lax.axis_size("band")
    _, blocks, times, _, directions, cells = coherencies.shape
    stations = gains.shape[3]
    plan = Plan(directions, stations, pairs, blocks, times, cells)
    k, zn = plan.k, plan.zn
    tile_count = stations * pairs // TILE
    step_size = 0.25 * tile_count * k / (times * TILE * blocks * pairs)

    vmem = pl.BlockSpec(memory_space=pltpu.VMEM)
    hbm = pl.BlockSpec(memory_space=pltpu.HBM)
    stay = lambda value: pltpu.with_memory_space_constraint(value, pltpu.HBM)
    i32 = lambda *shape: jax.ShapeDtypeStruct(shape, jnp.int32)
    f32 = lambda *shape: jax.ShapeDtypeStruct(shape, jnp.float32)
    scratch = [
        pltpu.VMEM((blocks, 2, k, LANES), jnp.float32),
        pltpu.VMEM((plan.total, 2, k, LANES), jnp.float32),
        pltpu.VMEM((blocks, 2, k, LANES), jnp.float32),
        pltpu.VMEM((blocks * PIECES * k, 2 * cells), jnp.bfloat16),
        pltpu.VMEM((2, 8 * times, LANES), jnp.float32),
        pltpu.VMEM((2, 3, 8, LANES), jnp.float32),
    ]
    params = pltpu.CompilerParams(vmem_limit_bytes=16 << 20)

    payload, meta, bounds, mult_rec = pl.pallas_call(
        lambda *refs: pack_kernel(plan, *refs),
        name="pack",
        in_specs=[hbm] * 5,
        out_specs=[vmem] * 4,
        out_shape=[f32(plan.rows, LANES), i32(8, LANES), i32(blocks, 2, 8, LANES), f32(k, LANES)],
        scratch_shapes=[pltpu.VMEM(gains.shape, jnp.float32)] * 3
        + [
            pltpu.VMEM(block_tiles.shape, jnp.int32),
            pltpu.VMEM((1, blocks), jnp.int32),
            pltpu.SemaphoreType.DMA((5,)),
        ],
        compiler_params=params,
    )(*map(stay, (block_tiles, sample_counts.reshape(1, blocks), gains, targets, multipliers)))

    vis, coh = pl.pallas_call(
        lambda *refs: load_kernel(plan, *refs),
        name="load",
        in_specs=[hbm] * 2,
        out_specs=[vmem] * 2,
        out_shape=[f32(plan.total, 2, times, LANES), f32(plan.total, times, 3, k, LANES)],
        scratch_shapes=[
            pltpu.VMEM((blocks, times, 2, cells), jnp.float32),
            pltpu.VMEM((blocks, times, 2, k, cells), jnp.bfloat16),
            pltpu.SemaphoreType.DMA((4 * blocks + 1,)),
        ],
        compiler_params=params,
    )(stay(visibilities), stay(coherencies))

    bf16 = lambda *shape: jax.ShapeDtypeStruct(shape, jnp.bfloat16)
    tables = pl.pallas_call(
        lambda *refs: table_kernel(plan, *refs),
        name="tables",
        in_specs=[],
        out_specs=[vmem] * 3,
        out_shape=[
            bf16(LANES, 2 * cells),
            bf16(2 * cells, LANES),
            bf16(2 * LANES, LANES),
        ],
        compiler_params=params,
    )()

    def gather(value):
        parts = [value] + [exchange(value, "pair", pairs, 2 * m) for m in range(1, zn)]
        own = jnp.stack(parts)
        return own, exchange(own, "pair", pairs, 1)

    own, sib = gather(payload)

    terms = pl.pallas_call(
        lambda *refs: first_kernel(plan, *refs),
        name="first",
        in_specs=[vmem] * 9,
        out_specs=vmem,
        out_shape=f32(blocks, k, LANES),
        scratch_shapes=scratch,
        compiler_params=params,
    )(meta, bounds, own, sib, vis, coh, *tables)

    term_own, term_sib = gather(terms)
    records, mine = pl.pallas_call(
        lambda *refs: near_kernel(plan, step_size, *refs),
        name="near",
        in_specs=[vmem] * 4,
        out_specs=[vmem] * 2,
        out_shape=[f32(2 * blocks, k, LANES), f32(max(plan.per, 1), k, LANES)],
        compiler_params=params,
    )(meta, own, sib, term_own)
    part_own, part_sib = pl.pallas_call(
        lambda *refs: second_kernel(plan, step_size, *refs),
        name="second",
        in_specs=[vmem] * 10,
        out_specs=[vmem] * 2,
        out_shape=[f32(zn, k, LANES)] * 2,
        scratch_shapes=scratch,
        compiler_params=params,
    )(meta, bounds, sib, term_sib, records, vis, coh, *tables)

    rest = pl.pallas_call(
        lambda *refs: rest_kernel(plan, step_size, *refs),
        name="rest",
        in_specs=[vmem] * 5,
        out_specs=vmem,
        out_shape=f32(2, k, LANES),
        compiler_params=params,
    )(own, sib, term_sib, mine, mult_rec)
    crossed = exchange(part_sib, "pair", pairs, 1)
    total = part_own[0] + crossed[0]
    for m in range(1, zn):
        total = total + exchange(part_own[m] + crossed[m], "pair", pairs, 2 * m)
    new_gain = rest[0] + step_size * total
    summed = rest[1] + step_size * total

    others = [exchange(summed, "band", bands, m) for m in range(1, bands)]
    shape = f32(*gains.shape)
    return pl.pallas_call(
        lambda *refs: fit_kernel(plan, fit_matrix(bands, P_SIZE), *refs),
        name="fit",
        in_specs=[vmem] * (2 + len(others)),
        out_specs=[vmem] * 3,
        out_shape=[shape] * 3,
        compiler_params=params,
    )(new_gain, summed, *others)


def solution(mesh):
    placed = (
        P("band", "pair", None, None, None),
        P("band", "pair", None, None, None, None),
        P("pair", None),
        P("pair"),
        P("band", None, None, "pair"),
        P("band", None, None, "pair"),
        P("band", None, None, "pair"),
    )
    return jax.shard_map(
        local,
        mesh=mesh,
        in_specs=placed,
        out_specs=(
            P("band", None, None, "pair"),
            P("band", None, None, "pair"),
            P("band", None, None, "pair"),
        ),
        check_vma=False,
    )
```

profile of v0, /device:TPU:0, one launch (start us, length us, event | category | flops | bytes accessed | tf_op | source)
XLA Modules:
  0.0 43.3 jit_solution(10204799459199410966)
XLA Ops:
  0.6 0.9 %pack.1 = (f32[72,128]{1,0:T(8,128)S(1)}, s32[8,128]{1,0:T(8,128)S(1)}, s32[2,2,8,128]{3,2,1,0:T(8,128)S(1)}, f32[32,128]{1,0:T(8,128)S(1)}) custom-call(s32[2,2]{1,0:T(2,128)} %refs_0_.2, s32[1,2]{1,0:T(1,128)} %bitcast.42, f32[1,2,32,64]{3,2,1,0:T(8,128)} %refs_2_.1, f32[1,2,32,64]{3,2,1,0:T(8,128)} %refs_3_.1, f32[1,2,32,64]{3,2,1,0:T(8,128)} %refs_4_.1), custom_call_target="tpu_custom_call" | custom-call | tf_op jit(solution)/shard_map/pack/pallas_call | solution.py:462
  1.6 5.1 %collective-permute-start.2 = (f32[72,128]{1,0:T(8,128)S(1)}, f32[72,128]{1,0:T(8,128)S(1)}, u32[]{:S(2)}, u32[]{:S(2)}) collective-permute-start(f32[72,128]{1,0:T(8,128)S(1)} %get-tuple-element.16), channel_id=1, source_target_pairs={{0,6},{1,7},{2,4},{3,5},{4,2},{5,3},{6,0},{7,1},{8,14},{9,15},{10,... | collective-permute-start | bytes 110600 | tf_op jit(solution)/shard_map/ppermute | solution.py:434
  6.7 0.0 collective-permute-start.1
  6.7 0.6 %collective-permute-start = (f32[72,128]{1,0:T(8,128)S(1)}, f32[72,128]{1,0:T(8,128)S(1)}, u32[]{:S(2)}, u32[]{:S(2)}) collective-permute-start(f32[72,128]{1,0:T(8,128)S(1)} %get-tuple-element.16), channel_id=1, source_target_pairs={{0,2},{1,3},{2,0},{3,1},{4,6},{5,7},{6,4},{7,5},{8,10},{9,11},{10,... | collective-permute-start | bytes 110600 | tf_op jit(solution)/shard_map/ppermute | solution.py:434
  7.4 1.3 %collective-permute-done.2 = f32[72,128]{1,0:T(8,128)S(1)} collective-permute-done((f32[72,128]{1,0:T(8,128)S(1)}, f32[72,128]{1,0:T(8,128)S(1)}, u32[]{:S(2)}, u32[]{:S(2)}) %collective-permute-start.2) | collective-permute-done | bytes 36896 | tf_op jit(solution)/shard_map/ppermute | solution.py:434
  8.7 2.9 %collective-permute-done.1 = f32[72,128]{1,0:T(8,128)S(1)} collective-permute-done((f32[72,128]{1,0:T(8,128)S(1)}, f32[72,128]{1,0:T(8,128)S(1)}, u32[]{:S(2)}, u32[]{:S(2)}) %collective-permute-start.1) | collective-permute-done | bytes 36896 | tf_op jit(solution)/shard_map/ppermute | solution.py:434
  11.6 0.0 collective-permute-done
  11.6 0.1 collective-permute-start.3
  11.7 0.2 tables.1
  11.9 1.8 %load.1 = (f32[16,2,8,128]{3,2,1,0:T(8,128)S(1)}, f32[16,8,3,32,128]{4,3,2,1,0:T(8,128)S(1)}) custom-call(f32[1,2,8,2,1024]{4,3,2,1,0:T(2,128)} %refs_0_.3, bf16[1,2,8,2,32,1024]{5,4,3,2,1,0:T(8,128)(2,1)} %refs_1_.1), custom_call_target="tpu_custom_call" | custom-call | tf_op jit(solution)/shard_map/load/pallas_call | solution.py:477
  13.7 0.0 collective-permute-done.3.refs_3_.refs_2_.refs_1_
  13.7 2.2 %first.1 = f32[2,32,128]{2,1,0:T(8,128)S(1)} custom-call(s32[8,128]{1,0:T(8,128)S(1)} %get-tuple-element.17.refs_0_, s32[2,2,8,128]{3,2,1,0:T(8,128)S(1)} %get-tuple-element.18.refs_1_, f32[4,72,128]{2,1,0:T(8,128)S(1)} %pad_maximum_fusion.refs_2_.refs_1_.refs_0_, f32[4,72,128]{2,1,0:T(8,128)S(1)} %collective-permute-done.3.refs_3_.refs_2_.refs_1_, ...), custom_call_target="tpu_custom_call" | custom-call | tf_op jit(solution)/shard_map/first/pallas_call | solution.py:512
  15.9 1.5 %collective-permute-start.6 = (f32[2,32,128]{2,1,0:T(8,128)S(1)}, f32[2,32,128]{2,1,0:T(8,128)S(1)}, u32[]{:S(2)}, u32[]{:S(2)}) collective-permute-start(f32[2,32,128]{2,1,0:T(8,128)S(1)} %first.1), channel_id=1, source_target_pairs={{0,6},{1,7},{2,4},{3,5},{4,2},{5,3},{6,0},{7,1},{8,14},{9,15},{10,... | collective-permute-start | bytes 98312 | tf_op jit(solution)/shard_map/ppermute | solution.py:434
  17.4 0.6 %collective-permute-start.5 = (f32[2,32,128]{2,1,0:T(8,128)S(1)}, f32[2,32,128]{2,1,0:T(8,128)S(1)}, u32[]{:S(2)}, u32[]{:S(2)}) collective-permute-start(f32[2,32,128]{2,1,0:T(8,128)S(1)} %first.1), channel_id=1, source_target_pairs={{0,4},{1,5},{2,6},{3,7},{4,0},{5,1},{6,2},{7,3},{8,12},{9,13},{10,... | collective-permute-start | bytes 98312 | tf_op jit(solution)/shard_map/ppermute | solution.py:434
  18.1 2.3 %collective-permute-start.4 = (f32[2,32,128]{2,1,0:T(8,128)S(1)}, f32[2,32,128]{2,1,0:T(8,128)S(1)}, u32[]{:S(2)}, u32[]{:S(2)}) collective-permute-start(f32[2,32,128]{2,1,0:T(8,128)S(1)} %first.1), channel_id=1, source_target_pairs={{0,2},{1,3},{2,0},{3,1},{4,6},{5,7},{6,4},{7,5},{8,10},{9,11},{10,... | collective-permute-start | bytes 98312 | tf_op jit(solution)/shard_map/ppermute | solution.py:434
  20.4 1.4 %collective-permute-done.6 = f32[2,32,128]{2,1,0:T(8,128)S(1)} collective-permute-done((f32[2,32,128]{2,1,0:T(8,128)S(1)}, f32[2,32,128]{2,1,0:T(8,128)S(1)}, u32[]{:S(2)}, u32[]{:S(2)}) %collective-permute-start.6) | collective-permute-done | bytes 32800 | tf_op jit(solution)/shard_map/ppermute | solution.py:434
  21.7 1.0 %collective-permute-done.5 = f32[2,32,128]{2,1,0:T(8,128)S(1)} collective-permute-done((f32[2,32,128]{2,1,0:T(8,128)S(1)}, f32[2,32,128]{2,1,0:T(8,128)S(1)}, u32[]{:S(2)}, u32[]{:S(2)}) %collective-permute-start.5) | collective-permute-done | bytes 32800 | tf_op jit(solution)/shard_map/ppermute | solution.py:434
  22.8 0.2 collective-permute-done.4
  23.0 0.1 collective-permute-start.7
  23.0 0.2 near.1
  23.3 1.1 %collective-permute-done.7.refs_2_.refs_3_ = f32[4,2,32,128]{3,2,1,0:T(8,128)S(1)} collective-permute-done((f32[4,2,32,128]{3,2,1,0:T(8,128)S(1)}, f32[4,2,32,128]{3,2,1,0:T(8,128)S(1)}, u32[]{:S(2)}, u32[]{:S(2)}) %collective-permute-start.7) | collective-permute-done | bytes 131104 | tf_op jit(solution)/shard_map/ppermute | solution.py:434
  24.4 2.2 %second.1 = (f32[4,32,128]{2,1,0:T(8,128)S(1)}, f32[4,32,128]{2,1,0:T(8,128)S(1)}) custom-call(s32[8,128]{1,0:T(8,128)S(1)} %get-tuple-element.17.refs_0_, s32[2,2,8,128]{3,2,1,0:T(8,128)S(1)} %get-tuple-element.18.refs_1_, f32[4,72,128]{2,1,0:T(8,128)S(1)} %collective-permute-done.3.refs_3_.refs_2_.refs_1_, ...), custom_call_target="tpu_custom_call" | custom-call | tf_op jit(solution)/shard_map/second/pallas_call | solution.py:531
  26.6 0.2 collective-permute-start.8
  26.8 1.1 %collective-permute-done.8 = f32[4,32,128]{2,1,0:T(8,128)S(1)} collective-permute-done((f32[4,32,128]{2,1,0:T(8,128)S(1)}, f32[4,32,128]{2,1,0:T(8,128)S(1)}, u32[]{:S(2)}, u32[]{:S(2)}) %collective-permute-start.8) | collective-permute-done | bytes 65568 | tf_op jit(solution)/shard_map/ppermute | solution.py:434
  28.0 2.2 %collective-permute-start.11 = (f32[32,128]{1,0:T(8,128)S(1)}, f32[32,128]{1,0:T(8,128)S(1)}, u32[]{:S(2)}, u32[]{:S(2)}) collective-permute-start(f32[32,128]{1,0:T(8,128)S(1)} %get-tuple-element.32), channel_id=1, source_target_pairs={{0,6},{1,7},{2,4},{3,5},{4,2},{5,3},{6,0},{7,1},{8,14},{9,15},{10,... | collective-permute-start | bytes 49160 | tf_op jit(solution)/shard_map/ppermute | solution.py:434
  30.2 0.6 %collective-permute-start.10 = (f32[32,128]{1,0:T(8,128)S(1)}, f32[32,128]{1,0:T(8,128)S(1)}, u32[]{:S(2)}, u32[]{:S(2)}) collective-permute-start(f32[32,128]{1,0:T(8,128)S(1)} %get-tuple-element.33), channel_id=1, source_target_pairs={{0,4},{1,5},{2,6},{3,7},{4,0},{5,1},{6,2},{7,3},{8,12},{9,13},{10,... | collective-permute-start | bytes 49160 | tf_op jit(solution)/shard_map/ppermute | solution.py:434
  30.8 1.6 %collective-permute-start.9 = (f32[32,128]{1,0:T(8,128)S(1)}, f32[32,128]{1,0:T(8,128)S(1)}, u32[]{:S(2)}, u32[]{:S(2)}) collective-permute-start(f32[32,128]{1,0:T(8,128)S(1)} %get-tuple-element.31), channel_id=1, source_target_pairs={{0,2},{1,3},{2,0},{3,1},{4,6},{5,7},{6,4},{7,5},{8,10},{9,11},{10,... | collective-permute-start | bytes 49160 | tf_op jit(solution)/shard_map/ppermute | solution.py:434
  32.4 0.2 rest.1
  32.6 1.0 %collective-permute-done.11 = f32[32,128]{1,0:T(8,128)S(1)} collective-permute-done((f32[32,128]{1,0:T(8,128)S(1)}, f32[32,128]{1,0:T(8,128)S(1)}, u32[]{:S(2)}, u32[]{:S(2)}) %collective-permute-start.11) | collective-permute-done | bytes 16416 | tf_op jit(solution)/shard_map/ppermute | solution.py:434
  33.6 1.3 %collective-permute-done.10 = f32[32,128]{1,0:T(8,128)S(1)} collective-permute-done((f32[32,128]{1,0:T(8,128)S(1)}, f32[32,128]{1,0:T(8,128)S(1)}, u32[]{:S(2)}, u32[]{:S(2)}) %collective-permute-start.10) | collective-permute-done | bytes 16416 | tf_op jit(solution)/shard_map/ppermute | solution.py:434
  34.8 0.0 collective-permute-done.9
  34.9 1.5 %collective-permute-start.12 = (f32[32,128]{1,0:T(8,128)S(1)}, f32[32,128]{1,0:T(8,128)S(1)}, u32[]{:S(2)}, u32[]{:S(2)}) collective-permute-start(f32[32,128]{1,0:T(8,128)S(1)} %get-tuple-element.29.refs_1_), channel_id=1, source_target_pairs={{0,8},{8,0},{16,24},{24,16},{1,9},{9,1},{17,25},{25,17},{2,10},{10... | collective-permute-start | bytes 49160 | tf_op jit(solution)/shard_map/ppermute | solution.py:434
  36.4 1.5 %collective-permute-start.13 = (f32[32,128]{1,0:T(8,128)S(1)}, f32[32,128]{1,0:T(8,128)S(1)}, u32[]{:S(2)}, u32[]{:S(2)}) collective-permute-start(f32[32,128]{1,0:T(8,128)S(1)} %get-tuple-element.29.refs_1_), channel_id=1, source_target_pairs={{0,16},{8,24},{16,0},{24,8},{1,17},{9,25},{17,1},{25,9},{2,18},{10... | collective-permute-start | bytes 49160 | tf_op jit(solution)/shard_map/ppermute | solution.py:434
  37.9 0.5 %collective-permute-start.14 = (f32[32,128]{1,0:T(8,128)S(1)}, f32[32,128]{1,0:T(8,128)S(1)}, u32[]{:S(2)}, u32[]{:S(2)}) collective-permute-start(f32[32,128]{1,0:T(8,128)S(1)} %get-tuple-element.29.refs_1_), channel_id=1, source_target_pairs={{0,24},{8,16},{16,8},{24,0},{1,25},{9,17},{17,9},{25,1},{2,26},{10... | collective-permute-start | bytes 49160 | tf_op jit(solution)/shard_map/ppermute | solution.py:434
  38.4 0.2 collective-permute-done.12.refs_2_
  38.7 1.5 %collective-permute-done.13.refs_3_ = f32[32,128]{1,0:T(8,128)S(1)} collective-permute-done((f32[32,128]{1,0:T(8,128)S(1)}, f32[32,128]{1,0:T(8,128)S(1)}, u32[]{:S(2)}, u32[]{:S(2)}) %collective-permute-start.13) | collective-permute-done | bytes 16416 | tf_op jit(solution)/shard_map/ppermute | solution.py:434
  40.1 2.4 %collective-permute-done.14.refs_4_ = f32[32,128]{1,0:T(8,128)S(1)} collective-permute-done((f32[32,128]{1,0:T(8,128)S(1)}, f32[32,128]{1,0:T(8,128)S(1)}, u32[]{:S(2)}, u32[]{:S(2)}) %collective-permute-start.14) | collective-permute-done | bytes 16416 | tf_op jit(solution)/shard_map/ppermute | solution.py:434
  42.6 0.7 %fit.1 = (f32[1,2,32,64]{3,2,1,0:T(8,128)}, f32[1,2,32,64]{3,2,1,0:T(8,128)}, f32[1,2,32,64]{3,2,1,0:T(8,128)}) custom-call(f32[32,128]{1,0:T(8,128)S(1)} %fusion.9.refs_0_, f32[32,128]{1,0:T(8,128)S(1)} %get-tuple-element.29.refs_1_, f32[32,128]{1,0:T(8,128)S(1)} %collective-permute-done.12.refs_2_, f32[32,128]{1,0:T(8,128)S(1)} %collective-permute-done.13.refs_3_, ...), custom_call_target="tpu_custom_call" | custom-call | tf_op jit(solution)/shard_map/fit/pallas_call | solution.py:558
  (5 shorter events, 0.0 us)
Async XLA Ops:
  1.6 7.1 %collective-permute-start.2 = (f32[72,128]{1,0:T(8,128)S(1)}, f32[72,128]{1,0:T(8,128)S(1)}, u32[]{:S(2)}, u32[]{:S(2)}) collective-permute-start(f32[72,128]{1,0:T(8,128)S(1)} %get-tuple-element.16), channel_id=1, source_target_pairs={{0,6},{1,7},{2,4},{3,5},{4,2},{5,3},{6,0},{7,1},{8,14},{9,15},{10,... | collective-permute-start | bytes 110600 | tf_op jit(solution)/shard_map/ppermute | solution.py:434
  6.7 4.9 %collective-permute-start.1 = (f32[72,128]{1,0:T(8,128)S(1)}, f32[72,128]{1,0:T(8,128)S(1)}, u32[]{:S(2)}, u32[]{:S(2)}) collective-permute-start(f32[72,128]{1,0:T(8,128)S(1)} %get-tuple-element.16), channel_id=1, source_target_pairs={{0,4},{1,5},{2,6},{3,7},{4,0},{5,1},{6,2},{7,3},{8,12},{9,13},{10,... | collective-permute-start | bytes 110600 | tf_op jit(solution)/shard_map/ppermute | solution.py:434
  6.7 4.9 %collective-permute-start = (f32[72,128]{1,0:T(8,128)S(1)}, f32[72,128]{1,0:T(8,128)S(1)}, u32[]{:S(2)}, u32[]{:S(2)}) collective-permute-start(f32[72,128]{1,0:T(8,128)S(1)} %get-tuple-element.16), channel_id=1, source_target_pairs={{0,2},{1,3},{2,0},{3,1},{4,6},{5,7},{6,4},{7,5},{8,10},{9,11},{10,... | collective-permute-start | bytes 110600 | tf_op jit(solution)/shard_map/ppermute | solution.py:434
  11.6 2.1 %collective-permute-start.3 = (f32[4,72,128]{2,1,0:T(8,128)S(1)}, f32[4,72,128]{2,1,0:T(8,128)S(1)}, u32[]{:S(2)}, u32[]{:S(2)}) collective-permute-start(f32[4,72,128]{2,1,0:T(8,128)S(1)} %pad_maximum_fusion.refs_2_.refs_1_.refs_0_), channel_id=1, source_target_pairs={{0,1},{1,0},{2,3},{3,2},{4,5},{5,4},{6,7},{7,6},{8,9},{9,8},{10,11... | collective-permute-start | bytes 442376 | tf_op jit(solution)/shard_map/ppermute | solution.py:434
  15.9 5.8 %collective-permute-start.6 = (f32[2,32,128]{2,1,0:T(8,128)S(1)}, f32[2,32,128]{2,1,0:T(8,128)S(1)}, u32[]{:S(2)}, u32[]{:S(2)}) collective-permute-start(f32[2,32,128]{2,1,0:T(8,128)S(1)} %first.1), channel_id=1, source_target_pairs={{0,6},{1,7},{2,4},{3,5},{4,2},{5,3},{6,0},{7,1},{8,14},{9,15},{10,... | collective-permute-start | bytes 98312 | tf_op jit(solution)/shard_map/ppermute | solution.py:434
  17.4 5.3 %collective-permute-start.5 = (f32[2,32,128]{2,1,0:T(8,128)S(1)}, f32[2,32,128]{2,1,0:T(8,128)S(1)}, u32[]{:S(2)}, u32[]{:S(2)}) collective-permute-start(f32[2,32,128]{2,1,0:T(8,128)S(1)} %first.1), channel_id=1, source_target_pairs={{0,4},{1,5},{2,6},{3,7},{4,0},{5,1},{6,2},{7,3},{8,12},{9,13},{10,... | collective-permute-start | bytes 98312 | tf_op jit(solution)/shard_map/ppermute | solution.py:434
  18.1 4.9 %collective-permute-start.4 = (f32[2,32,128]{2,1,0:T(8,128)S(1)}, f32[2,32,128]{2,1,0:T(8,128)S(1)}, u32[]{:S(2)}, u32[]{:S(2)}) collective-permute-start(f32[2,32,128]{2,1,0:T(8,128)S(1)} %first.1), channel_id=1, source_target_pairs={{0,2},{1,3},{2,0},{3,1},{4,6},{5,7},{6,4},{7,5},{8,10},{9,11},{10,... | collective-permute-start | bytes 98312 | tf_op jit(solution)/shard_map/ppermute | solution.py:434
  23.0 1.4 %collective-permute-start.7 = (f32[4,2,32,128]{3,2,1,0:T(8,128)S(1)}, f32[4,2,32,128]{3,2,1,0:T(8,128)S(1)}, u32[]{:S(2)}, u32[]{:S(2)}) collective-permute-start(f32[4,2,32,128]{3,2,1,0:T(8,128)S(1)} %pad_maximum_fusion.1.refs_3_), channel_id=1, source_target_pairs={{0,1},{1,0},{2,3},{3,2},{4,5},{5,4},{6,7},{7,6},{8,9},{9,8},{10,11... | collective-permute-start | bytes 393224 | tf_op jit(solution)/shard_map/ppermute | solution.py:434
  26.6 1.3 %collective-permute-start.8 = (f32[4,32,128]{2,1,0:T(8,128)S(1)}, f32[4,32,128]{2,1,0:T(8,128)S(1)}, u32[]{:S(2)}, u32[]{:S(2)}) collective-permute-start(f32[4,32,128]{2,1,0:T(8,128)S(1)} %get-tuple-element.28), channel_id=1, source_target_pairs={{0,1},{1,0},{2,3},{3,2},{4,5},{5,4},{6,7},{7,6},{8,9},{9,8},{10,11... | collective-permute-start | bytes 196616 | tf_op jit(solution)/shard_map/ppermute | solution.py:434
  28.0 5.6 %collective-permute-start.11 = (f32[32,128]{1,0:T(8,128)S(1)}, f32[32,128]{1,0:T(8,128)S(1)}, u32[]{:S(2)}, u32[]{:S(2)}) collective-permute-start(f32[32,128]{1,0:T(8,128)S(1)} %get-tuple-element.32), channel_id=1, source_target_pairs={{0,6},{1,7},{2,4},{3,5},{4,2},{5,3},{6,0},{7,1},{8,14},{9,15},{10,... | collective-permute-start | bytes 49160 | tf_op jit(solution)/shard_map/ppermute | solution.py:434
  30.2 4.6 %collective-permute-start.10 = (f32[32,128]{1,0:T(8,128)S(1)}, f32[32,128]{1,0:T(8,128)S(1)}, u32[]{:S(2)}, u32[]{:S(2)}) collective-permute-start(f32[32,128]{1,0:T(8,128)S(1)} %get-tuple-element.33), channel_id=1, source_target_pairs={{0,4},{1,5},{2,6},{3,7},{4,0},{5,1},{6,2},{7,3},{8,12},{9,13},{10,... | collective-permute-start | bytes 49160 | tf_op jit(solution)/shard_map/ppermute | solution.py:434
  30.8 4.0 %collective-permute-start.9 = (f32[32,128]{1,0:T(8,128)S(1)}, f32[32,128]{1,0:T(8,128)S(1)}, u32[]{:S(2)}, u32[]{:S(2)}) collective-permute-start(f32[32,128]{1,0:T(8,128)S(1)} %get-tuple-element.31), channel_id=1, source_target_pairs={{0,2},{1,3},{2,0},{3,1},{4,6},{5,7},{6,4},{7,5},{8,10},{9,11},{10,... | collective-permute-start | bytes 49160 | tf_op jit(solution)/shard_map/ppermute | solution.py:434
  34.9 3.8 %collective-permute-start.12 = (f32[32,128]{1,0:T(8,128)S(1)}, f32[32,128]{1,0:T(8,128)S(1)}, u32[]{:S(2)}, u32[]{:S(2)}) collective-permute-start(f32[32,128]{1,0:T(8,128)S(1)} %get-tuple-element.29.refs_1_), channel_id=1, source_target_pairs={{0,8},{8,0},{16,24},{24,16},{1,9},{9,1},{17,25},{25,17},{2,10},{10... | collective-permute-start | bytes 49160 | tf_op jit(solution)/shard_map/ppermute | solution.py:434
  36.4 3.7 %collective-permute-start.13 = (f32[32,128]{1,0:T(8,128)S(1)}, f32[32,128]{1,0:T(8,128)S(1)}, u32[]{:S(2)}, u32[]{:S(2)}) collective-permute-start(f32[32,128]{1,0:T(8,128)S(1)} %get-tuple-element.29.refs_1_), channel_id=1, source_target_pairs={{0,16},{8,24},{16,0},{24,8},{1,17},{9,25},{17,1},{25,9},{2,18},{10... | collective-permute-start | bytes 49160 | tf_op jit(solution)/shard_map/ppermute | solution.py:434
  37.9 4.6 %collective-permute-start.14 = (f32[32,128]{1,0:T(8,128)S(1)}, f32[32,128]{1,0:T(8,128)S(1)}, u32[]{:S(2)}, u32[]{:S(2)}) collective-permute-start(f32[32,128]{1,0:T(8,128)S(1)} %get-tuple-element.29.refs_1_), channel_id=1, source_target_pairs={{0,24},{8,16},{16,8},{24,0},{1,25},{9,17},{17,9},{25,1},{2,26},{10... | collective-permute-start | bytes 49160 | tf_op jit(solution)/shard_map/ppermute | solution.py:434
where the time goes:
time: 43.5 us; the launch traced here: 43.3 us
  starting transfers between devices  18.6 us (43%)
  waiting for transfers between devices  15.4 us (35%)
  Pallas kernels  8.48 us (19%)
  between operations  0.72 us (2%)
    ppermute x15, starting transfers between devices, exchange(): return lax.ppermute(value, axis, [(i, i ^ mask) for i in range(size)])  18.6 us
    ppermute x15, waiting for transfers between devices, exchange(): return lax.ppermute(value, axis, [(i, i ^ mask) for i in range(size)])  15.4 us
    pallas_call x1, Pallas kernels, local(): pl.pallas_call(lambda *refs: second_kernel(plan, step_size, *refs), name=...  2.25 us
    pallas_call x1, Pallas kernels, local(): pl.pallas_call(lambda *refs: first_kernel(plan, *refs), name='first', in_...  2.16 us
    pallas_call x1, Pallas kernels, local(): pl.pallas_call(lambda *refs: load_kernel(plan, *refs), name='load', in_sp...  1.78 us
    pallas_call x1, Pallas kernels, local(): pl.pallas_call(lambda *refs: pack_kernel(plan, *refs), name='pack', in_sp...  0.94 us
  transfers between devices with their start and end apart: 15, of which 12 were waited for; matrix products, arithmetic and copies ran while one was open for 0% of the time, Pallas kernels for 6%

commit v1 on v0

--- a/solution.py
+++ b/solution.py
@@ -56,7 +56,9 @@
         return lax.broadcasted_iota(jnp.int32, (self.k if rows is None else rows, LANES), 1)
 
     def owner(self, me, device):
-        return (device % 2) == (me % 2), (device // 2) ^ (me // 2)
+        slot = lax.shift_right_logical(device ^ me, 1)
+        crossed = lax.bitwise_and(device ^ me, 1)
+        return crossed == jnp.where(slot == 0, 0, 1), slot
 
     def record(self, me, own_ref, sib_ref, device, row):
         same, slot = self.owner(me, device)
@@ -503,7 +505,7 @@
     )()
 
     def gather(value):
-        parts = [value] + [exchange(value, "pair", pairs, 2 * m) for m in range(1, zn)]
+        parts = [value] + [exchange(value, "pair", pairs, 2 * m + 1) for m in range(1, zn)]
         own = jnp.stack(parts)
         return own, exchange(own, "pair", pairs, 1)
 
@@ -549,7 +551,7 @@
     crossed = exchange(part_sib, "pair", pairs, 1)
     total = part_own[0] + crossed[0]
     for m in range(1, zn):
-        total = total + exchange(part_own[m] + crossed[m], "pair", pairs, 2 * m)
+        total = total + exchange(part_own[m] + crossed[m], "pair", pairs, 2 * m + 1)
     new_gain = rest[0] + step_size * total
     summed = rest[1] + step_size * total
 

time: 43.5 us -> 42.1 us (0.968)
  starting transfers between devices: 18.6 us -> 17.7 us
  waiting for transfers between devices: 15.4 us -> 14.9 us
    ppermute x15, starting transfers between devices: 18.6 us -> 17.7 us  [exchange(): return lax.ppermute(value, axis, [(i, i ^ mask) for i in range(size)])]
    ppermute x15, waiting for transfers between devices: 15.4 us -> 14.9 us  [exchange(): return lax.ppermute(value, axis, [(i, i ^ mask) for i in range(size)])]
  transfers between devices with their start and end apart: 15 -> 15, of which waited for: 12 -> 11; matrix products, arithmetic and copies ran while one was open for 0% -> 0% of each run, Pallas kernels for 6% -> 6%
where the time goes in v1:
time: 42.1 us; the launch traced here: 41.9 us
  starting transfers between devices  17.7 us (42%)
  waiting for transfers between devices  14.9 us (35%)
  Pallas kernels  8.47 us (20%)
  between operations  0.71 us (2%)
    ppermute x15, starting transfers between devices, exchange(): return lax.ppermute(value, axis, [(i, i ^ mask) for i in range(size)])  17.7 us
    ppermute x15, waiting for transfers between devices, exchange(): return lax.ppermute(value, axis, [(i, i ^ mask) for i in range(size)])  14.9 us
    pallas_call x1, Pallas kernels, local(): pl.pallas_call(lambda *refs: second_kernel(plan, step_size, *refs), name=...  2.24 us
    pallas_call x1, Pallas kernels, local(): pl.pallas_call(lambda *refs: first_kernel(plan, *refs), name='first', in_...  2.16 us
    pallas_call x1, Pallas kernels, local(): pl.pallas_call(lambda *refs: load_kernel(plan, *refs), name='load', in_sp...  1.78 us
    pallas_call x1, Pallas kernels, local(): pl.pallas_call(lambda *refs: pack_kernel(plan, *refs), name='pack', in_sp...  0.94 us
  transfers between devices with their start and end apart: 15, of which 11 were waited for; matrix products, arithmetic and copies ran while one was open for 0% of the time, Pallas kernels for 6%

profile of v1, /device:TPU:0, one launch (start us, length us, event | category | flops | bytes accessed | tf_op | source)
XLA Modules:
  0.0 41.9 jit_solution(2849562810154928355)
XLA Ops:
  0.6 0.9 %pack.1 = (f32[72,128]{1,0:T(8,128)S(1)}, s32[8,128]{1,0:T(8,128)S(1)}, s32[2,2,8,128]{3,2,1,0:T(8,128)S(1)}, f32[32,128]{1,0:T(8,128)S(1)}) custom-call(s32[2,2]{1,0:T(2,128)} %refs_0_.2, s32[1,2]{1,0:T(1,128)} %bitcast.42, f32[1,2,32,64]{3,2,1,0:T(8,128)} %refs_2_.1, f32[1,2,32,64]{3,2,1,0:T(8,128)} %refs_3_.1, f32[1,2,32,64]{3,2,1,0:T(8,128)} %refs_4_.1), custom_call_target="tpu_custom_call" | custom-call | tf_op jit(solution)/shard_map/pack/pallas_call | solution.py:464
  1.6 4.6 %collective-permute-start.2 = (f32[72,128]{1,0:T(8,128)S(1)}, f32[72,128]{1,0:T(8,128)S(1)}, u32[]{:S(2)}, u32[]{:S(2)}) collective-permute-start(f32[72,128]{1,0:T(8,128)S(1)} %get-tuple-element.16), channel_id=1, source_target_pairs={{0,7},{1,6},{2,5},{3,4},{4,3},{5,2},{6,1},{7,0},{8,15},{9,14},{10,... | collective-permute-start | bytes 110600 | tf_op jit(solution)/shard_map/ppermute | solution.py:436
  6.2 0.0 collective-permute-start.1
  6.2 0.9 %collective-permute-start = (f32[72,128]{1,0:T(8,128)S(1)}, f32[72,128]{1,0:T(8,128)S(1)}, u32[]{:S(2)}, u32[]{:S(2)}) collective-permute-start(f32[72,128]{1,0:T(8,128)S(1)} %get-tuple-element.16), channel_id=1, source_target_pairs={{0,3},{1,2},{2,1},{3,0},{4,7},{5,6},{6,5},{7,4},{8,11},{9,10},{10,... | collective-permute-start | bytes 110600 | tf_op jit(solution)/shard_map/ppermute | solution.py:436
  7.1 0.9 %collective-permute-done.2 = f32[72,128]{1,0:T(8,128)S(1)} collective-permute-done((f32[72,128]{1,0:T(8,128)S(1)}, f32[72,128]{1,0:T(8,128)S(1)}, u32[]{:S(2)}, u32[]{:S(2)}) %collective-permute-start.2) | collective-permute-done | bytes 36896 | tf_op jit(solution)/shard_map/ppermute | solution.py:436
  8.0 2.8 %collective-permute-done.1 = f32[72,128]{1,0:T(8,128)S(1)} collective-permute-done((f32[72,128]{1,0:T(8,128)S(1)}, f32[72,128]{1,0:T(8,128)S(1)}, u32[]{:S(2)}, u32[]{:S(2)}) %collective-permute-start.1) | collective-permute-done | bytes 36896 | tf_op jit(solution)/shard_map/ppermute | solution.py:436
  10.8 0.0 collective-permute-done
  10.8 0.4 collective-permute-start.3
  11.2 0.2 tables.1
  11.5 1.8 %load.1 = (f32[16,2,8,128]{3,2,1,0:T(8,128)S(1)}, f32[16,8,3,32,128]{4,3,2,1,0:T(8,128)S(1)}) custom-call(f32[1,2,8,2,1024]{4,3,2,1,0:T(2,128)} %refs_0_.3, bf16[1,2,8,2,32,1024]{5,4,3,2,1,0:T(8,128)(2,1)} %refs_1_.1), custom_call_target="tpu_custom_call" | custom-call | tf_op jit(solution)/shard_map/load/pallas_call | solution.py:479
  13.2 0.0 collective-permute-done.3.refs_3_.refs_2_.refs_1_
  13.3 2.2 %first.1 = f32[2,32,128]{2,1,0:T(8,128)S(1)} custom-call(s32[8,128]{1,0:T(8,128)S(1)} %get-tuple-element.17.refs_0_, s32[2,2,8,128]{3,2,1,0:T(8,128)S(1)} %get-tuple-element.18.refs_1_, f32[4,72,128]{2,1,0:T(8,128)S(1)} %pad_maximum_fusion.refs_2_.refs_1_.refs_0_, f32[4,72,128]{2,1,0:T(8,128)S(1)} %collective-permute-done.3.refs_3_.refs_2_.refs_1_, ...), custom_call_target="tpu_custom_call" | custom-call | tf_op jit(solution)/shard_map/first/pallas_call | solution.py:514
  15.4 2.0 %collective-permute-start.6 = (f32[2,32,128]{2,1,0:T(8,128)S(1)}, f32[2,32,128]{2,1,0:T(8,128)S(1)}, u32[]{:S(2)}, u32[]{:S(2)}) collective-permute-start(f32[2,32,128]{2,1,0:T(8,128)S(1)} %first.1), channel_id=1, source_target_pairs={{0,7},{1,6},{2,5},{3,4},{4,3},{5,2},{6,1},{7,0},{8,15},{9,14},{10,... | collective-permute-start | bytes 98312 | tf_op jit(solution)/shard_map/ppermute | solution.py:436
  17.5 0.3 collective-permute-start.5
  17.7 1.6 %collective-permute-start.4 = (f32[2,32,128]{2,1,0:T(8,128)S(1)}, f32[2,32,128]{2,1,0:T(8,128)S(1)}, u32[]{:S(2)}, u32[]{:S(2)}) collective-permute-start(f32[2,32,128]{2,1,0:T(8,128)S(1)} %first.1), channel_id=1, source_target_pairs={{0,3},{1,2},{2,1},{3,0},{4,7},{5,6},{6,5},{7,4},{8,11},{9,10},{10,... | collective-permute-start | bytes 98312 | tf_op jit(solution)/shard_map/ppermute | solution.py:436
  19.4 1.3 %collective-permute-done.6 = f32[2,32,128]{2,1,0:T(8,128)S(1)} collective-permute-done((f32[2,32,128]{2,1,0:T(8,128)S(1)}, f32[2,32,128]{2,1,0:T(8,128)S(1)}, u32[]{:S(2)}, u32[]{:S(2)}) %collective-permute-start.6) | collective-permute-done | bytes 32800 | tf_op jit(solution)/shard_map/ppermute | solution.py:436
  20.6 1.9 %collective-permute-done.5 = f32[2,32,128]{2,1,0:T(8,128)S(1)} collective-permute-done((f32[2,32,128]{2,1,0:T(8,128)S(1)}, f32[2,32,128]{2,1,0:T(8,128)S(1)}, u32[]{:S(2)}, u32[]{:S(2)}) %collective-permute-start.5) | collective-permute-done | bytes 32800 | tf_op jit(solution)/shard_map/ppermute | solution.py:436
  22.5 0.0 collective-permute-done.4
  22.5 0.2 collective-permute-start.7
  22.7 0.2 near.1
  22.9 1.0 %collective-permute-done.7.refs_2_.refs_3_ = f32[4,2,32,128]{3,2,1,0:T(8,128)S(1)} collective-permute-done((f32[4,2,32,128]{3,2,1,0:T(8,128)S(1)}, f32[4,2,32,128]{3,2,1,0:T(8,128)S(1)}, u32[]{:S(2)}, u32[]{:S(2)}) %collective-permute-start.7) | collective-permute-done | bytes 131104 | tf_op jit(solution)/shard_map/ppermute | solution.py:436
  24.0 2.2 %second.1 = (f32[4,32,128]{2,1,0:T(8,128)S(1)}, f32[4,32,128]{2,1,0:T(8,128)S(1)}) custom-call(s32[8,128]{1,0:T(8,128)S(1)} %get-tuple-element.17.refs_0_, s32[2,2,8,128]{3,2,1,0:T(8,128)S(1)} %get-tuple-element.18.refs_1_, f32[4,72,128]{2,1,0:T(8,128)S(1)} %collective-permute-done.3.refs_3_.refs_2_.refs_1_, ...), custom_call_target="tpu_custom_call" | custom-call | tf_op jit(solution)/shard_map/second/pallas_call | solution.py:533
  26.2 0.2 collective-permute-start.8
  26.4 1.1 %collective-permute-done.8 = f32[4,32,128]{2,1,0:T(8,128)S(1)} collective-permute-done((f32[4,32,128]{2,1,0:T(8,128)S(1)}, f32[4,32,128]{2,1,0:T(8,128)S(1)}, u32[]{:S(2)}, u32[]{:S(2)}) %collective-permute-start.8) | collective-permute-done | bytes 65568 | tf_op jit(solution)/shard_map/ppermute | solution.py:436
  27.5 1.8 %collective-permute-start.11 = (f32[32,128]{1,0:T(8,128)S(1)}, f32[32,128]{1,0:T(8,128)S(1)}, u32[]{:S(2)}, u32[]{:S(2)}) collective-permute-start(f32[32,128]{1,0:T(8,128)S(1)} %get-tuple-element.32), channel_id=1, source_target_pairs={{0,7},{1,6},{2,5},{3,4},{4,3},{5,2},{6,1},{7,0},{8,15},{9,14},{10,... | collective-permute-start | bytes 49160 | tf_op jit(solution)/shard_map/ppermute | solution.py:436
  29.4 0.0 collective-permute-start.10
  29.4 2.1 %collective-permute-start.9 = (f32[32,128]{1,0:T(8,128)S(1)}, f32[32,128]{1,0:T(8,128)S(1)}, u32[]{:S(2)}, u32[]{:S(2)}) collective-permute-start(f32[32,128]{1,0:T(8,128)S(1)} %get-tuple-element.31), channel_id=1, source_target_pairs={{0,3},{1,2},{2,1},{3,0},{4,7},{5,6},{6,5},{7,4},{8,11},{9,10},{10,... | collective-permute-start | bytes 49160 | tf_op jit(solution)/shard_map/ppermute | solution.py:436
  31.5 0.2 rest.1
  31.6 0.9 %collective-permute-done.11 = f32[32,128]{1,0:T(8,128)S(1)} collective-permute-done((f32[32,128]{1,0:T(8,128)S(1)}, f32[32,128]{1,0:T(8,128)S(1)}, u32[]{:S(2)}, u32[]{:S(2)}) %collective-permute-start.11) | collective-permute-done | bytes 16416 | tf_op jit(solution)/shard_map/ppermute | solution.py:436
  32.6 0.9 %collective-permute-done.10 = f32[32,128]{1,0:T(8,128)S(1)} collective-permute-done((f32[32,128]{1,0:T(8,128)S(1)}, f32[32,128]{1,0:T(8,128)S(1)}, u32[]{:S(2)}, u32[]{:S(2)}) %collective-permute-start.10) | collective-permute-done | bytes 16416 | tf_op jit(solution)/shard_map/ppermute | solution.py:436
  33.4 0.0 collective-permute-done.9
  33.5 1.6 %collective-permute-start.12 = (f32[32,128]{1,0:T(8,128)S(1)}, f32[32,128]{1,0:T(8,128)S(1)}, u32[]{:S(2)}, u32[]{:S(2)}) collective-permute-start(f32[32,128]{1,0:T(8,128)S(1)} %get-tuple-element.29.refs_1_), channel_id=1, source_target_pairs={{0,8},{8,0},{16,24},{24,16},{1,9},{9,1},{17,25},{25,17},{2,10},{10... | collective-permute-start | bytes 49160 | tf_op jit(solution)/shard_map/ppermute | solution.py:436
  35.0 1.5 %collective-permute-start.13 = (f32[32,128]{1,0:T(8,128)S(1)}, f32[32,128]{1,0:T(8,128)S(1)}, u32[]{:S(2)}, u32[]{:S(2)}) collective-permute-start(f32[32,128]{1,0:T(8,128)S(1)} %get-tuple-element.29.refs_1_), channel_id=1, source_target_pairs={{0,16},{8,24},{16,0},{24,8},{1,17},{9,25},{17,1},{25,9},{2,18},{10... | collective-permute-start | bytes 49160 | tf_op jit(solution)/shard_map/ppermute | solution.py:436
  36.5 0.5 %collective-permute-start.14 = (f32[32,128]{1,0:T(8,128)S(1)}, f32[32,128]{1,0:T(8,128)S(1)}, u32[]{:S(2)}, u32[]{:S(2)}) collective-permute-start(f32[32,128]{1,0:T(8,128)S(1)} %get-tuple-element.29.refs_1_), channel_id=1, source_target_pairs={{0,24},{8,16},{16,8},{24,0},{1,25},{9,17},{17,9},{25,1},{2,26},{10... | collective-permute-start | bytes 49160 | tf_op jit(solution)/shard_map/ppermute | solution.py:436
  37.0 0.2 collective-permute-done.12.refs_2_
  37.3 1.5 %collective-permute-done.13.refs_3_ = f32[32,128]{1,0:T(8,128)S(1)} collective-permute-done((f32[32,128]{1,0:T(8,128)S(1)}, f32[32,128]{1,0:T(8,128)S(1)}, u32[]{:S(2)}, u32[]{:S(2)}) %collective-permute-start.13) | collective-permute-done | bytes 16416 | tf_op jit(solution)/shard_map/ppermute | solution.py:436
  38.8 2.4 %collective-permute-done.14.refs_4_ = f32[32,128]{1,0:T(8,128)S(1)} collective-permute-done((f32[32,128]{1,0:T(8,128)S(1)}, f32[32,128]{1,0:T(8,128)S(1)}, u32[]{:S(2)}, u32[]{:S(2)}) %collective-permute-start.14) | collective-permute-done | bytes 16416 | tf_op jit(solution)/shard_map/ppermute | solution.py:436
  41.2 0.7 %fit.1 = (f32[1,2,32,64]{3,2,1,0:T(8,128)}, f32[1,2,32,64]{3,2,1,0:T(8,128)}, f32[1,2,32,64]{3,2,1,0:T(8,128)}) custom-call(f32[32,128]{1,0:T(8,128)S(1)} %fusion.9.refs_0_, f32[32,128]{1,0:T(8,128)S(1)} %get-tuple-element.29.refs_1_, f32[32,128]{1,0:T(8,128)S(1)} %collective-permute-done.12.refs_2_, f32[32,128]{1,0:T(8,128)S(1)} %collective-permute-done.13.refs_3_, ...), custom_call_target="tpu_custom_call" | custom-call | tf_op jit(solution)/shard_map/fit/pallas_call | solution.py:560
  (5 shorter events, 0.0 us)
Async XLA Ops:
  1.6 6.5 %collective-permute-start.2 = (f32[72,128]{1,0:T(8,128)S(1)}, f32[72,128]{1,0:T(8,128)S(1)}, u32[]{:S(2)}, u32[]{:S(2)}) collective-permute-start(f32[72,128]{1,0:T(8,128)S(1)} %get-tuple-element.16), channel_id=1, source_target_pairs={{0,7},{1,6},{2,5},{3,4},{4,3},{5,2},{6,1},{7,0},{8,15},{9,14},{10,... | collective-permute-start | bytes 110600 | tf_op jit(solution)/shard_map/ppermute | solution.py:436
  6.2 4.6 %collective-permute-start.1 = (f32[72,128]{1,0:T(8,128)S(1)}, f32[72,128]{1,0:T(8,128)S(1)}, u32[]{:S(2)}, u32[]{:S(2)}) collective-permute-start(f32[72,128]{1,0:T(8,128)S(1)} %get-tuple-element.16), channel_id=1, source_target_pairs={{0,5},{1,4},{2,7},{3,6},{4,1},{5,0},{6,3},{7,2},{8,13},{9,12},{10,... | collective-permute-start | bytes 110600 | tf_op jit(solution)/shard_map/ppermute | solution.py:436
  6.2 4.6 %collective-permute-start = (f32[72,128]{1,0:T(8,128)S(1)}, f32[72,128]{1,0:T(8,128)S(1)}, u32[]{:S(2)}, u32[]{:S(2)}) collective-permute-start(f32[72,128]{1,0:T(8,128)S(1)} %get-tuple-element.16), channel_id=1, source_target_pairs={{0,3},{1,2},{2,1},{3,0},{4,7},{5,6},{6,5},{7,4},{8,11},{9,10},{10,... | collective-permute-start | bytes 110600 | tf_op jit(solution)/shard_map/ppermute | solution.py:436
  10.8 2.4 %collective-permute-start.3 = (f32[4,72,128]{2,1,0:T(8,128)S(1)}, f32[4,72,128]{2,1,0:T(8,128)S(1)}, u32[]{:S(2)}, u32[]{:S(2)}) collective-permute-start(f32[4,72,128]{2,1,0:T(8,128)S(1)} %pad_maximum_fusion.refs_2_.refs_1_.refs_0_), channel_id=1, source_target_pairs={{0,1},{1,0},{2,3},{3,2},{4,5},{5,4},{6,7},{7,6},{8,9},{9,8},{10,11... | collective-permute-start | bytes 442376 | tf_op jit(solution)/shard_map/ppermute | solution.py:436
  15.4 5.2 %collective-permute-start.6 = (f32[2,32,128]{2,1,0:T(8,128)S(1)}, f32[2,32,128]{2,1,0:T(8,128)S(1)}, u32[]{:S(2)}, u32[]{:S(2)}) collective-permute-start(f32[2,32,128]{2,1,0:T(8,128)S(1)} %first.1), channel_id=1, source_target_pairs={{0,7},{1,6},{2,5},{3,4},{4,3},{5,2},{6,1},{7,0},{8,15},{9,14},{10,... | collective-permute-start | bytes 98312 | tf_op jit(solution)/shard_map/ppermute | solution.py:436
  17.5 5.1 %collective-permute-start.5 = (f32[2,32,128]{2,1,0:T(8,128)S(1)}, f32[2,32,128]{2,1,0:T(8,128)S(1)}, u32[]{:S(2)}, u32[]{:S(2)}) collective-permute-start(f32[2,32,128]{2,1,0:T(8,128)S(1)} %first.1), channel_id=1, source_target_pairs={{0,5},{1,4},{2,7},{3,6},{4,1},{5,0},{6,3},{7,2},{8,13},{9,12},{10,... | collective-permute-start | bytes 98312 | tf_op jit(solution)/shard_map/ppermute | solution.py:436
  17.7 4.8 %collective-permute-start.4 = (f32[2,32,128]{2,1,0:T(8,128)S(1)}, f32[2,32,128]{2,1,0:T(8,128)S(1)}, u32[]{:S(2)}, u32[]{:S(2)}) collective-permute-start(f32[2,32,128]{2,1,0:T(8,128)S(1)} %first.1), channel_id=1, source_target_pairs={{0,3},{1,2},{2,1},{3,0},{4,7},{5,6},{6,5},{7,4},{8,11},{9,10},{10,... | collective-permute-start | bytes 98312 | tf_op jit(solution)/shard_map/ppermute | solution.py:436
  22.5 1.4 %collective-permute-start.7 = (f32[4,2,32,128]{3,2,1,0:T(8,128)S(1)}, f32[4,2,32,128]{3,2,1,0:T(8,128)S(1)}, u32[]{:S(2)}, u32[]{:S(2)}) collective-permute-start(f32[4,2,32,128]{3,2,1,0:T(8,128)S(1)} %pad_maximum_fusion.1.refs_3_), channel_id=1, source_target_pairs={{0,1},{1,0},{2,3},{3,2},{4,5},{5,4},{6,7},{7,6},{8,9},{9,8},{10,11... | collective-permute-start | bytes 393224 | tf_op jit(solution)/shard_map/ppermute | solution.py:436
  26.2 1.3 %collective-permute-start.8 = (f32[4,32,128]{2,1,0:T(8,128)S(1)}, f32[4,32,128]{2,1,0:T(8,128)S(1)}, u32[]{:S(2)}, u32[]{:S(2)}) collective-permute-start(f32[4,32,128]{2,1,0:T(8,128)S(1)} %get-tuple-element.28), channel_id=1, source_target_pairs={{0,1},{1,0},{2,3},{3,2},{4,5},{5,4},{6,7},{7,6},{8,9},{9,8},{10,11... | collective-permute-start | bytes 196616 | tf_op jit(solution)/shard_map/ppermute | solution.py:436
  27.5 5.0 %collective-permute-start.11 = (f32[32,128]{1,0:T(8,128)S(1)}, f32[32,128]{1,0:T(8,128)S(1)}, u32[]{:S(2)}, u32[]{:S(2)}) collective-permute-start(f32[32,128]{1,0:T(8,128)S(1)} %get-tuple-element.32), channel_id=1, source_target_pairs={{0,7},{1,6},{2,5},{3,4},{4,3},{5,2},{6,1},{7,0},{8,15},{9,14},{10,... | collective-permute-start | bytes 49160 | tf_op jit(solution)/shard_map/ppermute | solution.py:436
  29.4 4.1 %collective-permute-start.10 = (f32[32,128]{1,0:T(8,128)S(1)}, f32[32,128]{1,0:T(8,128)S(1)}, u32[]{:S(2)}, u32[]{:S(2)}) collective-permute-start(f32[32,128]{1,0:T(8,128)S(1)} %get-tuple-element.33), channel_id=1, source_target_pairs={{0,5},{1,4},{2,7},{3,6},{4,1},{5,0},{6,3},{7,2},{8,13},{9,12},{10,... | collective-permute-start | bytes 49160 | tf_op jit(solution)/shard_map/ppermute | solution.py:436
  29.4 4.1 %collective-permute-start.9 = (f32[32,128]{1,0:T(8,128)S(1)}, f32[32,128]{1,0:T(8,128)S(1)}, u32[]{:S(2)}, u32[]{:S(2)}) collective-permute-start(f32[32,128]{1,0:T(8,128)S(1)} %get-tuple-element.31), channel_id=1, source_target_pairs={{0,3},{1,2},{2,1},{3,0},{4,7},{5,6},{6,5},{7,4},{8,11},{9,10},{10,... | collective-permute-start | bytes 49160 | tf_op jit(solution)/shard_map/ppermute | solution.py:436
  33.5 3.8 %collective-permute-start.12 = (f32[32,128]{1,0:T(8,128)S(1)}, f32[32,128]{1,0:T(8,128)S(1)}, u32[]{:S(2)}, u32[]{:S(2)}) collective-permute-start(f32[32,128]{1,0:T(8,128)S(1)} %get-tuple-element.29.refs_1_), channel_id=1, source_target_pairs={{0,8},{8,0},{16,24},{24,16},{1,9},{9,1},{17,25},{25,17},{2,10},{10... | collective-permute-start | bytes 49160 | tf_op jit(solution)/shard_map/ppermute | solution.py:436
  35.0 3.7 %collective-permute-start.13 = (f32[32,128]{1,0:T(8,128)S(1)}, f32[32,128]{1,0:T(8,128)S(1)}, u32[]{:S(2)}, u32[]{:S(2)}) collective-permute-start(f32[32,128]{1,0:T(8,128)S(1)} %get-tuple-element.29.refs_1_), channel_id=1, source_target_pairs={{0,16},{8,24},{16,0},{24,8},{1,17},{9,25},{17,1},{25,9},{2,18},{10... | collective-permute-start | bytes 49160 | tf_op jit(solution)/shard_map/ppermute | solution.py:436
  36.5 4.6 %collective-permute-start.14 = (f32[32,128]{1,0:T(8,128)S(1)}, f32[32,128]{1,0:T(8,128)S(1)}, u32[]{:S(2)}, u32[]{:S(2)}) collective-permute-start(f32[32,128]{1,0:T(8,128)S(1)} %get-tuple-element.29.refs_1_), channel_id=1, source_target_pairs={{0,24},{8,16},{16,8},{24,0},{1,25},{9,17},{17,9},{25,1},{2,26},{10... | collective-permute-start | bytes 49160 | tf_op jit(solution)/shard_map/ppermute | solution.py:436

commit v2 on v1

--- a/solution.py
+++ b/solution.py
@@ -243,11 +243,11 @@
     lane_k = plan.lane()
     lane = plan.lane(8)
     sample = lax.broadcasted_iota(jnp.int32, (8, LANES), 0)
-    lefts = [piece for left, _ in tile_gains for piece in pieces(left, 3)]
+    lefts = [piece for left, _ in tile_gains for piece in pieces(left, 2)]
     lefts = matmul(jnp.concatenate(lefts, axis=0), spread_ref[...])
     for n in range(plan.blocks):
-        rows = [lefts[(3 * n + i) * k : (3 * n + i + 1) * k] for i in range(3)]
-        value = rows[0] + rows[1] + rows[2]
+        rows = [lefts[(2 * n + i) * k : (2 * n + i + 1) * k] for i in range(2)]
+        value = rows[0] + rows[1]
         for index in range(steps):
             for part in range(2):
                 start = (2 * index + part) * LANES

time: 42.1 us -> 42 us (level)
  no operation moved by 1% of the time
where the time goes in v2:
time: 42 us; the launch traced here: 41.7 us
  starting transfers between devices  17.7 us (42%)
  waiting for transfers between devices  14.9 us (35%)
  Pallas kernels  8.32 us (20%)
  between operations  0.71 us (2%)
    ppermute x15, starting transfers between devices, exchange(): return lax.ppermute(value, axis, [(i, i ^ mask) for i in range(size)])  17.7 us
    ppermute x15, waiting for transfers between devices, exchange(): return lax.ppermute(value, axis, [(i, i ^ mask) for i in range(size)])  14.9 us
    pallas_call x1, Pallas kernels, local(): pl.pallas_call(lambda *refs: second_kernel(plan, step_size, *refs), name=...  2.18 us
    pallas_call x1, Pallas kernels, local(): pl.pallas_call(lambda *refs: first_kernel(plan, *refs), name='first', in_...  2.09 us
    pallas_call x1, Pallas kernels, local(): pl.pallas_call(lambda *refs: load_kernel(plan, *refs), name='load', in_sp...  1.78 us
    pallas_call x1, Pallas kernels, local(): pl.pallas_call(lambda *refs: pack_kernel(plan, *refs), name='pack', in_sp...  0.94 us
  transfers between devices with their start and end apart: 15, of which 11 were waited for; matrix products, arithmetic and copies ran while one was open for 0% of the time, Pallas kernels for 6%

profile of v2, /device:TPU:0, one launch (start us, length us, event | category | flops | bytes accessed | tf_op | source)
XLA Modules:
  0.0 41.7 jit_solution(1245285919168353313)
XLA Ops:
  0.6 0.9 %pack.1 = (f32[72,128]{1,0:T(8,128)S(1)}, s32[8,128]{1,0:T(8,128)S(1)}, s32[2,2,8,128]{3,2,1,0:T(8,128)S(1)}, f32[32,128]{1,0:T(8,128)S(1)}) custom-call(s32[2,2]{1,0:T(2,128)} %refs_0_.2, s32[1,2]{1,0:T(1,128)} %bitcast.42, f32[1,2,32,64]{3,2,1,0:T(8,128)} %refs_2_.1, f32[1,2,32,64]{3,2,1,0:T(8,128)} %refs_3_.1, f32[1,2,32,64]{3,2,1,0:T(8,128)} %refs_4_.1), custom_call_target="tpu_custom_call" | custom-call | tf_op jit(solution)/shard_map/pack/pallas_call | solution.py:464
  1.6 4.6 %collective-permute-start.2 = (f32[72,128]{1,0:T(8,128)S(1)}, f32[72,128]{1,0:T(8,128)S(1)}, u32[]{:S(2)}, u32[]{:S(2)}) collective-permute-start(f32[72,128]{1,0:T(8,128)S(1)} %get-tuple-element.16), channel_id=1, source_target_pairs={{0,7},{1,6},{2,5},{3,4},{4,3},{5,2},{6,1},{7,0},{8,15},{9,14},{10,... | collective-permute-start | bytes 110600 | tf_op jit(solution)/shard_map/ppermute | solution.py:436
  6.2 0.0 collective-permute-start.1
  6.2 0.9 %collective-permute-start = (f32[72,128]{1,0:T(8,128)S(1)}, f32[72,128]{1,0:T(8,128)S(1)}, u32[]{:S(2)}, u32[]{:S(2)}) collective-permute-start(f32[72,128]{1,0:T(8,128)S(1)} %get-tuple-element.16), channel_id=1, source_target_pairs={{0,3},{1,2},{2,1},{3,0},{4,7},{5,6},{6,5},{7,4},{8,11},{9,10},{10,... | collective-permute-start | bytes 110600 | tf_op jit(solution)/shard_map/ppermute | solution.py:436
  7.1 0.9 %collective-permute-done.2 = f32[72,128]{1,0:T(8,128)S(1)} collective-permute-done((f32[72,128]{1,0:T(8,128)S(1)}, f32[72,128]{1,0:T(8,128)S(1)}, u32[]{:S(2)}, u32[]{:S(2)}) %collective-permute-start.2) | collective-permute-done | bytes 36896 | tf_op jit(solution)/shard_map/ppermute | solution.py:436
  8.0 2.8 %collective-permute-done.1 = f32[72,128]{1,0:T(8,128)S(1)} collective-permute-done((f32[72,128]{1,0:T(8,128)S(1)}, f32[72,128]{1,0:T(8,128)S(1)}, u32[]{:S(2)}, u32[]{:S(2)}) %collective-permute-start.1) | collective-permute-done | bytes 36896 | tf_op jit(solution)/shard_map/ppermute | solution.py:436
  10.8 0.0 collective-permute-done
  10.8 0.4 collective-permute-start.3
  11.2 0.2 tables.1
  11.5 1.8 %load.1 = (f32[16,2,8,128]{3,2,1,0:T(8,128)S(1)}, f32[16,8,3,32,128]{4,3,2,1,0:T(8,128)S(1)}) custom-call(f32[1,2,8,2,1024]{4,3,2,1,0:T(2,128)} %refs_0_.3, bf16[1,2,8,2,32,1024]{5,4,3,2,1,0:T(8,128)(2,1)} %refs_1_.1), custom_call_target="tpu_custom_call" | custom-call | tf_op jit(solution)/shard_map/load/pallas_call | solution.py:479
  13.2 0.0 collective-permute-done.3.refs_3_.refs_2_.refs_1_
  13.3 2.1 %first.1 = f32[2,32,128]{2,1,0:T(8,128)S(1)} custom-call(s32[8,128]{1,0:T(8,128)S(1)} %get-tuple-element.17.refs_0_, s32[2,2,8,128]{3,2,1,0:T(8,128)S(1)} %get-tuple-element.18.refs_1_, f32[4,72,128]{2,1,0:T(8,128)S(1)} %pad_maximum_fusion.refs_2_.refs_1_.refs_0_, f32[4,72,128]{2,1,0:T(8,128)S(1)} %collective-permute-done.3.refs_3_.refs_2_.refs_1_, ...), custom_call_target="tpu_custom_call" | custom-call | tf_op jit(solution)/shard_map/first/pallas_call | solution.py:514
  15.3 2.1 %collective-permute-start.6 = (f32[2,32,128]{2,1,0:T(8,128)S(1)}, f32[2,32,128]{2,1,0:T(8,128)S(1)}, u32[]{:S(2)}, u32[]{:S(2)}) collective-permute-start(f32[2,32,128]{2,1,0:T(8,128)S(1)} %first.1), channel_id=1, source_target_pairs={{0,7},{1,6},{2,5},{3,4},{4,3},{5,2},{6,1},{7,0},{8,15},{9,14},{10,... | collective-permute-start | bytes 98312 | tf_op jit(solution)/shard_map/ppermute | solution.py:436
  17.4 0.2 collective-permute-start.5
  17.7 1.6 %collective-permute-start.4 = (f32[2,32,128]{2,1,0:T(8,128)S(1)}, f32[2,32,128]{2,1,0:T(8,128)S(1)}, u32[]{:S(2)}, u32[]{:S(2)}) collective-permute-start(f32[2,32,128]{2,1,0:T(8,128)S(1)} %first.1), channel_id=1, source_target_pairs={{0,3},{1,2},{2,1},{3,0},{4,7},{5,6},{6,5},{7,4},{8,11},{9,10},{10,... | collective-permute-start | bytes 98312 | tf_op jit(solution)/shard_map/ppermute | solution.py:436
  19.3 1.3 %collective-permute-done.6 = f32[2,32,128]{2,1,0:T(8,128)S(1)} collective-permute-done((f32[2,32,128]{2,1,0:T(8,128)S(1)}, f32[2,32,128]{2,1,0:T(8,128)S(1)}, u32[]{:S(2)}, u32[]{:S(2)}) %collective-permute-start.6) | collective-permute-done | bytes 32800 | tf_op jit(solution)/shard_map/ppermute | solution.py:436
  20.6 1.9 %collective-permute-done.5 = f32[2,32,128]{2,1,0:T(8,128)S(1)} collective-permute-done((f32[2,32,128]{2,1,0:T(8,128)S(1)}, f32[2,32,128]{2,1,0:T(8,128)S(1)}, u32[]{:S(2)}, u32[]{:S(2)}) %collective-permute-start.5) | collective-permute-done | bytes 32800 | tf_op jit(solution)/shard_map/ppermute | solution.py:436
  22.5 0.0 collective-permute-done.4
  22.5 0.2 collective-permute-start.7
  22.7 0.2 near.1
  22.9 1.0 %collective-permute-done.7.refs_2_.refs_3_ = f32[4,2,32,128]{3,2,1,0:T(8,128)S(1)} collective-permute-done((f32[4,2,32,128]{3,2,1,0:T(8,128)S(1)}, f32[4,2,32,128]{3,2,1,0:T(8,128)S(1)}, u32[]{:S(2)}, u32[]{:S(2)}) %collective-permute-start.7) | collective-permute-done | bytes 131104 | tf_op jit(solution)/shard_map/ppermute | solution.py:436
  23.9 2.2 %second.1 = (f32[4,32,128]{2,1,0:T(8,128)S(1)}, f32[4,32,128]{2,1,0:T(8,128)S(1)}) custom-call(s32[8,128]{1,0:T(8,128)S(1)} %get-tuple-element.17.refs_0_, s32[2,2,8,128]{3,2,1,0:T(8,128)S(1)} %get-tuple-element.18.refs_1_, f32[4,72,128]{2,1,0:T(8,128)S(1)} %collective-permute-done.3.refs_3_.refs_2_.refs_1_, ...), custom_call_target="tpu_custom_call" | custom-call | tf_op jit(solution)/shard_map/second/pallas_call | solution.py:533
  26.1 0.2 collective-permute-start.8
  26.3 1.1 %collective-permute-done.8 = f32[4,32,128]{2,1,0:T(8,128)S(1)} collective-permute-done((f32[4,32,128]{2,1,0:T(8,128)S(1)}, f32[4,32,128]{2,1,0:T(8,128)S(1)}, u32[]{:S(2)}, u32[]{:S(2)}) %collective-permute-start.8) | collective-permute-done | bytes 65568 | tf_op jit(solution)/shard_map/ppermute | solution.py:436
  27.4 1.8 %collective-permute-start.11 = (f32[32,128]{1,0:T(8,128)S(1)}, f32[32,128]{1,0:T(8,128)S(1)}, u32[]{:S(2)}, u32[]{:S(2)}) collective-permute-start(f32[32,128]{1,0:T(8,128)S(1)} %get-tuple-element.32), channel_id=1, source_target_pairs={{0,7},{1,6},{2,5},{3,4},{4,3},{5,2},{6,1},{7,0},{8,15},{9,14},{10,... | collective-permute-start | bytes 49160 | tf_op jit(solution)/shard_map/ppermute | solution.py:436
  29.2 0.0 collective-permute-start.10
  29.2 2.1 %collective-permute-start.9 = (f32[32,128]{1,0:T(8,128)S(1)}, f32[32,128]{1,0:T(8,128)S(1)}, u32[]{:S(2)}, u32[]{:S(2)}) collective-permute-start(f32[32,128]{1,0:T(8,128)S(1)} %get-tuple-element.31), channel_id=1, source_target_pairs={{0,3},{1,2},{2,1},{3,0},{4,7},{5,6},{6,5},{7,4},{8,11},{9,10},{10,... | collective-permute-start | bytes 49160 | tf_op jit(solution)/shard_map/ppermute | solution.py:436
  31.3 0.2 rest.1
  31.5 0.9 %collective-permute-done.11 = f32[32,128]{1,0:T(8,128)S(1)} collective-permute-done((f32[32,128]{1,0:T(8,128)S(1)}, f32[32,128]{1,0:T(8,128)S(1)}, u32[]{:S(2)}, u32[]{:S(2)}) %collective-permute-start.11) | collective-permute-done | bytes 16416 | tf_op jit(solution)/shard_map/ppermute | solution.py:436
  32.4 0.9 %collective-permute-done.10 = f32[32,128]{1,0:T(8,128)S(1)} collective-permute-done((f32[32,128]{1,0:T(8,128)S(1)}, f32[32,128]{1,0:T(8,128)S(1)}, u32[]{:S(2)}, u32[]{:S(2)}) %collective-permute-start.10) | collective-permute-done | bytes 16416 | tf_op jit(solution)/shard_map/ppermute | solution.py:436
  33.3 0.0 collective-permute-done.9
  33.3 1.6 %collective-permute-start.12 = (f32[32,128]{1,0:T(8,128)S(1)}, f32[32,128]{1,0:T(8,128)S(1)}, u32[]{:S(2)}, u32[]{:S(2)}) collective-permute-start(f32[32,128]{1,0:T(8,128)S(1)} %get-tuple-element.29.refs_1_), channel_id=1, source_target_pairs={{0,8},{8,0},{16,24},{24,16},{1,9},{9,1},{17,25},{25,17},{2,10},{10... | collective-permute-start | bytes 49160 | tf_op jit(solution)/shard_map/ppermute | solution.py:436
  34.9 1.5 %collective-permute-start.13 = (f32[32,128]{1,0:T(8,128)S(1)}, f32[32,128]{1,0:T(8,128)S(1)}, u32[]{:S(2)}, u32[]{:S(2)}) collective-permute-start(f32[32,128]{1,0:T(8,128)S(1)} %get-tuple-element.29.refs_1_), channel_id=1, source_target_pairs={{0,16},{8,24},{16,0},{24,8},{1,17},{9,25},{17,1},{25,9},{2,18},{10... | collective-permute-start | bytes 49160 | tf_op jit(solution)/shard_map/ppermute | solution.py:436
  36.4 0.5 %collective-permute-start.14 = (f32[32,128]{1,0:T(8,128)S(1)}, f32[32,128]{1,0:T(8,128)S(1)}, u32[]{:S(2)}, u32[]{:S(2)}) collective-permute-start(f32[32,128]{1,0:T(8,128)S(1)} %get-tuple-element.29.refs_1_), channel_id=1, source_target_pairs={{0,24},{8,16},{16,8},{24,0},{1,25},{9,17},{17,9},{25,1},{2,26},{10... | collective-permute-start | bytes 49160 | tf_op jit(solution)/shard_map/ppermute | solution.py:436
  36.9 0.2 collective-permute-done.12.refs_2_
  37.1 1.5 %collective-permute-done.13.refs_3_ = f32[32,128]{1,0:T(8,128)S(1)} collective-permute-done((f32[32,128]{1,0:T(8,128)S(1)}, f32[32,128]{1,0:T(8,128)S(1)}, u32[]{:S(2)}, u32[]{:S(2)}) %collective-permute-start.13) | collective-permute-done | bytes 16416 | tf_op jit(solution)/shard_map/ppermute | solution.py:436
  38.6 2.4 %collective-permute-done.14.refs_4_ = f32[32,128]{1,0:T(8,128)S(1)} collective-permute-done((f32[32,128]{1,0:T(8,128)S(1)}, f32[32,128]{1,0:T(8,128)S(1)}, u32[]{:S(2)}, u32[]{:S(2)}) %collective-permute-start.14) | collective-permute-done | bytes 16416 | tf_op jit(solution)/shard_map/ppermute | solution.py:436
  41.0 0.7 %fit.1 = (f32[1,2,32,64]{3,2,1,0:T(8,128)}, f32[1,2,32,64]{3,2,1,0:T(8,128)}, f32[1,2,32,64]{3,2,1,0:T(8,128)}) custom-call(f32[32,128]{1,0:T(8,128)S(1)} %fusion.9.refs_0_, f32[32,128]{1,0:T(8,128)S(1)} %get-tuple-element.29.refs_1_, f32[32,128]{1,0:T(8,128)S(1)} %collective-permute-done.12.refs_2_, f32[32,128]{1,0:T(8,128)S(1)} %collective-permute-done.13.refs_3_, ...), custom_call_target="tpu_custom_call" | custom-call | tf_op jit(solution)/shard_map/fit/pallas_call | solution.py:560
  (5 shorter events, 0.0 us)
Async XLA Ops:
  1.6 6.5 %collective-permute-start.2 = (f32[72,128]{1,0:T(8,128)S(1)}, f32[72,128]{1,0:T(8,128)S(1)}, u32[]{:S(2)}, u32[]{:S(2)}) collective-permute-start(f32[72,128]{1,0:T(8,128)S(1)} %get-tuple-element.16), channel_id=1, source_target_pairs={{0,7},{1,6},{2,5},{3,4},{4,3},{5,2},{6,1},{7,0},{8,15},{9,14},{10,... | collective-permute-start | bytes 110600 | tf_op jit(solution)/shard_map/ppermute | solution.py:436
  6.2 4.6 %collective-permute-start.1 = (f32[72,128]{1,0:T(8,128)S(1)}, f32[72,128]{1,0:T(8,128)S(1)}, u32[]{:S(2)}, u32[]{:S(2)}) collective-permute-start(f32[72,128]{1,0:T(8,128)S(1)} %get-tuple-element.16), channel_id=1, source_target_pairs={{0,5},{1,4},{2,7},{3,6},{4,1},{5,0},{6,3},{7,2},{8,13},{9,12},{10,... | collective-permute-start | bytes 110600 | tf_op jit(solution)/shard_map/ppermute | solution.py:436
  6.2 4.6 %collective-permute-start = (f32[72,128]{1,0:T(8,128)S(1)}, f32[72,128]{1,0:T(8,128)S(1)}, u32[]{:S(2)}, u32[]{:S(2)}) collective-permute-start(f32[72,128]{1,0:T(8,128)S(1)} %get-tuple-element.16), channel_id=1, source_target_pairs={{0,3},{1,2},{2,1},{3,0},{4,7},{5,6},{6,5},{7,4},{8,11},{9,10},{10,... | collective-permute-start | bytes 110600 | tf_op jit(solution)/shard_map/ppermute | solution.py:436
  10.8 2.4 %collective-permute-start.3 = (f32[4,72,128]{2,1,0:T(8,128)S(1)}, f32[4,72,128]{2,1,0:T(8,128)S(1)}, u32[]{:S(2)}, u32[]{:S(2)}) collective-permute-start(f32[4,72,128]{2,1,0:T(8,128)S(1)} %pad_maximum_fusion.refs_2_.refs_1_.refs_0_), channel_id=1, source_target_pairs={{0,1},{1,0},{2,3},{3,2},{4,5},{5,4},{6,7},{7,6},{8,9},{9,8},{10,11... | collective-permute-start | bytes 442376 | tf_op jit(solution)/shard_map/ppermute | solution.py:436
  15.3 5.2 %collective-permute-start.6 = (f32[2,32,128]{2,1,0:T(8,128)S(1)}, f32[2,32,128]{2,1,0:T(8,128)S(1)}, u32[]{:S(2)}, u32[]{:S(2)}) collective-permute-start(f32[2,32,128]{2,1,0:T(8,128)S(1)} %first.1), channel_id=1, source_target_pairs={{0,7},{1,6},{2,5},{3,4},{4,3},{5,2},{6,1},{7,0},{8,15},{9,14},{10,... | collective-permute-start | bytes 98312 | tf_op jit(solution)/shard_map/ppermute | solution.py:436
  17.4 5.1 %collective-permute-start.5 = (f32[2,32,128]{2,1,0:T(8,128)S(1)}, f32[2,32,128]{2,1,0:T(8,128)S(1)}, u32[]{:S(2)}, u32[]{:S(2)}) collective-permute-start(f32[2,32,128]{2,1,0:T(8,128)S(1)} %first.1), channel_id=1, source_target_pairs={{0,5},{1,4},{2,7},{3,6},{4,1},{5,0},{6,3},{7,2},{8,13},{9,12},{10,... | collective-permute-start | bytes 98312 | tf_op jit(solution)/shard_map/ppermute | solution.py:436
  17.7 4.8 %collective-permute-start.4 = (f32[2,32,128]{2,1,0:T(8,128)S(1)}, f32[2,32,128]{2,1,0:T(8,128)S(1)}, u32[]{:S(2)}, u32[]{:S(2)}) collective-permute-start(f32[2,32,128]{2,1,0:T(8,128)S(1)} %first.1), channel_id=1, source_target_pairs={{0,3},{1,2},{2,1},{3,0},{4,7},{5,6},{6,5},{7,4},{8,11},{9,10},{10,... | collective-permute-start | bytes 98312 | tf_op jit(solution)/shard_map/ppermute | solution.py:436
  22.5 1.4 %collective-permute-start.7 = (f32[4,2,32,128]{3,2,1,0:T(8,128)S(1)}, f32[4,2,32,128]{3,2,1,0:T(8,128)S(1)}, u32[]{:S(2)}, u32[]{:S(2)}) collective-permute-start(f32[4,2,32,128]{3,2,1,0:T(8,128)S(1)} %pad_maximum_fusion.1.refs_3_), channel_id=1, source_target_pairs={{0,1},{1,0},{2,3},{3,2},{4,5},{5,4},{6,7},{7,6},{8,9},{9,8},{10,11... | collective-permute-start | bytes 393224 | tf_op jit(solution)/shard_map/ppermute | solution.py:436
  26.1 1.3 %collective-permute-start.8 = (f32[4,32,128]{2,1,0:T(8,128)S(1)}, f32[4,32,128]{2,1,0:T(8,128)S(1)}, u32[]{:S(2)}, u32[]{:S(2)}) collective-permute-start(f32[4,32,128]{2,1,0:T(8,128)S(1)} %get-tuple-element.28), channel_id=1, source_target_pairs={{0,1},{1,0},{2,3},{3,2},{4,5},{5,4},{6,7},{7,6},{8,9},{9,8},{10,11... | collective-permute-start | bytes 196616 | tf_op jit(solution)/shard_map/ppermute | solution.py:436
  27.4 5.0 %collective-permute-start.11 = (f32[32,128]{1,0:T(8,128)S(1)}, f32[32,128]{1,0:T(8,128)S(1)}, u32[]{:S(2)}, u32[]{:S(2)}) collective-permute-start(f32[32,128]{1,0:T(8,128)S(1)} %get-tuple-element.32), channel_id=1, source_target_pairs={{0,7},{1,6},{2,5},{3,4},{4,3},{5,2},{6,1},{7,0},{8,15},{9,14},{10,... | collective-permute-start | bytes 49160 | tf_op jit(solution)/shard_map/ppermute | solution.py:436
  29.2 4.1 %collective-permute-start.10 = (f32[32,128]{1,0:T(8,128)S(1)}, f32[32,128]{1,0:T(8,128)S(1)}, u32[]{:S(2)}, u32[]{:S(2)}) collective-permute-start(f32[32,128]{1,0:T(8,128)S(1)} %get-tuple-element.33), channel_id=1, source_target_pairs={{0,5},{1,4},{2,7},{3,6},{4,1},{5,0},{6,3},{7,2},{8,13},{9,12},{10,... | collective-permute-start | bytes 49160 | tf_op jit(solution)/shard_map/ppermute | solution.py:436
  29.2 4.1 %collective-permute-start.9 = (f32[32,128]{1,0:T(8,128)S(1)}, f32[32,128]{1,0:T(8,128)S(1)}, u32[]{:S(2)}, u32[]{:S(2)}) collective-permute-start(f32[32,128]{1,0:T(8,128)S(1)} %get-tuple-element.31), channel_id=1, source_target_pairs={{0,3},{1,2},{2,1},{3,0},{4,7},{5,6},{6,5},{7,4},{8,11},{9,10},{10,... | collective-permute-start | bytes 49160 | tf_op jit(solution)/shard_map/ppermute | solution.py:436
  33.3 3.8 %collective-permute-start.12 = (f32[32,128]{1,0:T(8,128)S(1)}, f32[32,128]{1,0:T(8,128)S(1)}, u32[]{:S(2)}, u32[]{:S(2)}) collective-permute-start(f32[32,128]{1,0:T(8,128)S(1)} %get-tuple-element.29.refs_1_), channel_id=1, source_target_pairs={{0,8},{8,0},{16,24},{24,16},{1,9},{9,1},{17,25},{25,17},{2,10},{10... | collective-permute-start | bytes 49160 | tf_op jit(solution)/shard_map/ppermute | solution.py:436
  34.9 3.7 %collective-permute-start.13 = (f32[32,128]{1,0:T(8,128)S(1)}, f32[32,128]{1,0:T(8,128)S(1)}, u32[]{:S(2)}, u32[]{:S(2)}) collective-permute-start(f32[32,128]{1,0:T(8,128)S(1)} %get-tuple-element.29.refs_1_), channel_id=1, source_target_pairs={{0,16},{8,24},{16,0},{24,8},{1,17},{9,25},{17,1},{25,9},{2,18},{10... | collective-permute-start | bytes 49160 | tf_op jit(solution)/shard_map/ppermute | solution.py:436
  36.4 4.6 %collective-permute-start.14 = (f32[32,128]{1,0:T(8,128)S(1)}, f32[32,128]{1,0:T(8,128)S(1)}, u32[]{:S(2)}, u32[]{:S(2)}) collective-permute-start(f32[32,128]{1,0:T(8,128)S(1)} %get-tuple-element.29.refs_1_), channel_id=1, source_target_pairs={{0,24},{8,16},{16,8},{24,0},{1,25},{9,17},{17,9},{25,1},{2,26},{10... | collective-permute-start | bytes 49160 | tf_op jit(solution)/shard_map/ppermute | solution.py:436

commit v3 on v2

--- a/solution.py
+++ b/solution.py
@@ -177,7 +177,7 @@
 
 
 def load_kernel(plan, vis_hbm, coh_hbm, vis_ref, coh_ref, vis_buf, coh_buf, sems):
-    chunks = 4
+    chunks = 8
     per = plan.steps // chunks
     copies = []
     for n in range(plan.blocks):
@@ -412,8 +412,14 @@
             plan.spread(me, tiles[2 * n + side], terms, side, part_own_ref, part_sib_ref)
 
 
-def fit_kernel(plan, fit, gain_ref, own_ref, *refs):
-    others, (gain_out, target_out, mult_out) = refs[:-3], refs[-3:]
+def emit_kernel(plan, gain_ref, gain_out):
+    gain = gain_ref[...]
+    for part in range(2):
+        gain_out[0, part] = gain[:, part * plan.sl : (part + 1) * plan.sl]
+
+
+def fit_kernel(plan, fit, own_ref, *refs):
+    others, (target_out, mult_out) = refs[:-2], refs[-2:]
     sl = plan.sl
     band = lax.axis_index("band")
     total = None
@@ -424,10 +430,8 @@
         value = factor * ref[...]
         total = value if total is None else total + value
     change = own_ref[...] - total
-    gain = gain_ref[...]
     for part in range(2):
         lanes = slice(part * sl, (part + 1) * sl)
-        gain_out[0, part] = gain[:, lanes]
         target_out[0, part] = total[:, lanes]
         mult_out[0, part] = change[:, lanes]
 
@@ -485,7 +489,7 @@
         scratch_shapes=[
             pltpu.VMEM((blocks, times, 2, cells), jnp.float32),
             pltpu.VMEM((blocks, times, 2, k, cells), jnp.bfloat16),
-            pltpu.SemaphoreType.DMA((4 * blocks + 1,)),
+            pltpu.SemaphoreType.DMA((8 * blocks + 1,)),
         ],
         compiler_params=params,
     )(stay(visibilities), stay(coherencies))
@@ -556,15 +560,24 @@
     summed = rest[1] + step_size * total
 
     others = [exchange(summed, "band", bands, m) for m in range(1, bands)]
+    emitted = pl.pallas_call(
+        lambda *refs: emit_kernel(plan, *refs),
+        name="emit",
+        in_specs=[vmem],
+        out_specs=vmem,
+        out_shape=f32(*gains.shape),
+        compiler_params=params,
+    )(new_gain)
     shape = f32(*gains.shape)
-    return pl.pallas_call(
+    fitted, change = pl.pallas_call(
         lambda *refs: fit_kernel(plan, fit_matrix(bands, P_SIZE), *refs),
         name="fit",
-        in_specs=[vmem] * (2 + len(others)),
-        out_specs=[vmem] * 3,
-        out_shape=[shape] * 3,
-        compiler_params=params,
-    )(new_gain, summed, *others)
+        in_specs=[vmem] * (1 + len(others)),
+        out_specs=[vmem] * 2,
+        out_shape=[shape] * 2,
+        compiler_params=params,
+    )(summed, *others)
+    return emitted, fitted, change
 
 
 def solution(mesh):

time: 42 us -> 42.4 us (level)
  Pallas kernels: 8.32 us -> 9.41 us
  waiting for transfers between devices: 14.9 us -> 14.2 us
    pallas_call x0 -> x1, Pallas kernels: none -> 0.69 us  [local(): pl.pallas_call(lambda *refs: emit_kernel(plan, *refs), name='emit', in_sp...]
    ppermute x15, waiting for transfers between devices: 14.9 us -> 14.2 us  [exchange(): return lax.ppermute(value, axis, [(i, i ^ mask) for i in range(size)])]
  transfers between devices with their start and end apart: 15 -> 15, of which waited for: 11 -> 10; matrix products, arithmetic and copies ran while one was open for 0% -> 0% of each run, Pallas kernels for 6% -> 8%
where the time goes in v3:
time: 42.4 us; the launch traced here: 42.1 us
  starting transfers between devices  17.7 us (42%)
  waiting for transfers between devices  14.2 us (33%)
  Pallas kernels  9.41 us (22%)
  between operations  0.71 us (2%)
    ppermute x15, starting transfers between devices, exchange(): return lax.ppermute(value, axis, [(i, i ^ mask) for i in range(size)])  17.7 us
    ppermute x15, waiting for transfers between devices, exchange(): return lax.ppermute(value, axis, [(i, i ^ mask) for i in range(size)])  14.2 us
    pallas_call x1, Pallas kernels, local(): pl.pallas_call(lambda *refs: load_kernel(plan, *refs), name='load', in_sp...  2.19 us
    pallas_call x1, Pallas kernels, local(): pl.pallas_call(lambda *refs: second_kernel(plan, step_size, *refs), name=...  2.17 us
    pallas_call x1, Pallas kernels, local(): pl.pallas_call(lambda *refs: first_kernel(plan, *refs), name='first', in_...  2.08 us
    pallas_call x1, Pallas kernels, local(): pl.pallas_call(lambda *refs: pack_kernel(plan, *refs), name='pack', in_sp...  0.94 us
  transfers between devices with their start and end apart: 15, of which 10 were waited for; matrix products, arithmetic and copies ran while one was open for 0% of the time, Pallas kernels for 8%

profile of v3, /device:TPU:0, one launch (start us, length us, event | category | flops | bytes accessed | tf_op | source)
XLA Modules:
  0.0 42.1 jit_solution(149459461247238959)
XLA Ops:
  0.6 0.9 %pack.1 = (f32[72,128]{1,0:T(8,128)S(1)}, s32[8,128]{1,0:T(8,128)S(1)}, s32[2,2,8,128]{3,2,1,0:T(8,128)S(1)}, f32[32,128]{1,0:T(8,128)S(1)}) custom-call(s32[2,2]{1,0:T(2,128)} %refs_0_.2, s32[1,2]{1,0:T(1,128)} %bitcast.42, f32[1,2,32,64]{3,2,1,0:T(8,128)} %refs_2_.1, f32[1,2,32,64]{3,2,1,0:T(8,128)} %refs_3_.1, f32[1,2,32,64]{3,2,1,0:T(8,128)} %refs_4_.1), custom_call_target="tpu_custom_call" | custom-call | tf_op jit(solution)/shard_map/pack/pallas_call | solution.py:468
  1.6 4.6 %collective-permute-start.2 = (f32[72,128]{1,0:T(8,128)S(1)}, f32[72,128]{1,0:T(8,128)S(1)}, u32[]{:S(2)}, u32[]{:S(2)}) collective-permute-start(f32[72,128]{1,0:T(8,128)S(1)} %get-tuple-element.18), channel_id=1, source_target_pairs={{0,7},{1,6},{2,5},{3,4},{4,3},{5,2},{6,1},{7,0},{8,15},{9,14},{10,... | collective-permute-start | bytes 110600 | tf_op jit(solution)/shard_map/ppermute | solution.py:440
  6.2 0.0 collective-permute-start.1
  6.2 0.9 %collective-permute-start = (f32[72,128]{1,0:T(8,128)S(1)}, f32[72,128]{1,0:T(8,128)S(1)}, u32[]{:S(2)}, u32[]{:S(2)}) collective-permute-start(f32[72,128]{1,0:T(8,128)S(1)} %get-tuple-element.18), channel_id=1, source_target_pairs={{0,3},{1,2},{2,1},{3,0},{4,7},{5,6},{6,5},{7,4},{8,11},{9,10},{10,... | collective-permute-start | bytes 110600 | tf_op jit(solution)/shard_map/ppermute | solution.py:440
  7.1 0.9 %collective-permute-done.2 = f32[72,128]{1,0:T(8,128)S(1)} collective-permute-done((f32[72,128]{1,0:T(8,128)S(1)}, f32[72,128]{1,0:T(8,128)S(1)}, u32[]{:S(2)}, u32[]{:S(2)}) %collective-permute-start.2) | collective-permute-done | bytes 36896 | tf_op jit(solution)/shard_map/ppermute | solution.py:440
  8.0 2.8 %collective-permute-done.1 = f32[72,128]{1,0:T(8,128)S(1)} collective-permute-done((f32[72,128]{1,0:T(8,128)S(1)}, f32[72,128]{1,0:T(8,128)S(1)}, u32[]{:S(2)}, u32[]{:S(2)}) %collective-permute-start.1) | collective-permute-done | bytes 36896 | tf_op jit(solution)/shard_map/ppermute | solution.py:440
  10.8 0.0 collective-permute-done
  10.8 0.4 collective-permute-start.3
  11.2 0.2 tables.1
  11.5 2.2 %load.1 = (f32[16,2,8,128]{3,2,1,0:T(8,128)S(1)}, f32[16,8,3,32,128]{4,3,2,1,0:T(8,128)S(1)}) custom-call(f32[1,2,8,2,1024]{4,3,2,1,0:T(2,128)} %refs_0_.3, bf16[1,2,8,2,32,1024]{5,4,3,2,1,0:T(8,128)(2,1)} %refs_1_.1), custom_call_target="tpu_custom_call" | custom-call | tf_op jit(solution)/shard_map/load/pallas_call | solution.py:483
  13.7 0.0 collective-permute-done.3.refs_3_.refs_2_.refs_1_
  13.7 2.1 %first.1 = f32[2,32,128]{2,1,0:T(8,128)S(1)} custom-call(s32[8,128]{1,0:T(8,128)S(1)} %get-tuple-element.19.refs_0_, s32[2,2,8,128]{3,2,1,0:T(8,128)S(1)} %get-tuple-element.20.refs_1_, f32[4,72,128]{2,1,0:T(8,128)S(1)} %pad_maximum_fusion.refs_2_.refs_1_.refs_0_, f32[4,72,128]{2,1,0:T(8,128)S(1)} %collective-permute-done.3.refs_3_.refs_2_.refs_1_, ...), custom_call_target="tpu_custom_call" | custom-call | tf_op jit(solution)/shard_map/first/pallas_call | solution.py:518
  15.8 2.1 %collective-permute-start.6 = (f32[2,32,128]{2,1,0:T(8,128)S(1)}, f32[2,32,128]{2,1,0:T(8,128)S(1)}, u32[]{:S(2)}, u32[]{:S(2)}) collective-permute-start(f32[2,32,128]{2,1,0:T(8,128)S(1)} %first.1), channel_id=1, source_target_pairs={{0,7},{1,6},{2,5},{3,4},{4,3},{5,2},{6,1},{7,0},{8,15},{9,14},{10,... | collective-permute-start | bytes 98312 | tf_op jit(solution)/shard_map/ppermute | solution.py:440
  17.8 0.2 collective-permute-start.5
  18.1 1.6 %collective-permute-start.4 = (f32[2,32,128]{2,1,0:T(8,128)S(1)}, f32[2,32,128]{2,1,0:T(8,128)S(1)}, u32[]{:S(2)}, u32[]{:S(2)}) collective-permute-start(f32[2,32,128]{2,1,0:T(8,128)S(1)} %first.1), channel_id=1, source_target_pairs={{0,3},{1,2},{2,1},{3,0},{4,7},{5,6},{6,5},{7,4},{8,11},{9,10},{10,... | collective-permute-start | bytes 98312 | tf_op jit(solution)/shard_map/ppermute | solution.py:440
  19.7 1.3 %collective-permute-done.6 = f32[2,32,128]{2,1,0:T(8,128)S(1)} collective-permute-done((f32[2,32,128]{2,1,0:T(8,128)S(1)}, f32[2,32,128]{2,1,0:T(8,128)S(1)}, u32[]{:S(2)}, u32[]{:S(2)}) %collective-permute-start.6) | collective-permute-done | bytes 32800 | tf_op jit(solution)/shard_map/ppermute | solution.py:440
  21.0 1.9 %collective-permute-done.5 = f32[2,32,128]{2,1,0:T(8,128)S(1)} collective-permute-done((f32[2,32,128]{2,1,0:T(8,128)S(1)}, f32[2,32,128]{2,1,0:T(8,128)S(1)}, u32[]{:S(2)}, u32[]{:S(2)}) %collective-permute-start.5) | collective-permute-done | bytes 32800 | tf_op jit(solution)/shard_map/ppermute | solution.py:440
  22.9 0.0 collective-permute-done.4
  22.9 0.2 collective-permute-start.7
  23.1 0.2 near.1
  23.3 1.0 %collective-permute-done.7.refs_2_.refs_3_ = f32[4,2,32,128]{3,2,1,0:T(8,128)S(1)} collective-permute-done((f32[4,2,32,128]{3,2,1,0:T(8,128)S(1)}, f32[4,2,32,128]{3,2,1,0:T(8,128)S(1)}, u32[]{:S(2)}, u32[]{:S(2)}) %collective-permute-start.7) | collective-permute-done | bytes 131104 | tf_op jit(solution)/shard_map/ppermute | solution.py:440
  24.3 2.2 %second.1 = (f32[4,32,128]{2,1,0:T(8,128)S(1)}, f32[4,32,128]{2,1,0:T(8,128)S(1)}) custom-call(s32[8,128]{1,0:T(8,128)S(1)} %get-tuple-element.19.refs_0_, s32[2,2,8,128]{3,2,1,0:T(8,128)S(1)} %get-tuple-element.20.refs_1_, f32[4,72,128]{2,1,0:T(8,128)S(1)} %collective-permute-done.3.refs_3_.refs_2_.refs_1_, ...), custom_call_target="tpu_custom_call" | custom-call | tf_op jit(solution)/shard_map/second/pallas_call | solution.py:537
  26.5 0.2 collective-permute-start.8
  26.7 1.1 %collective-permute-done.8 = f32[4,32,128]{2,1,0:T(8,128)S(1)} collective-permute-done((f32[4,32,128]{2,1,0:T(8,128)S(1)}, f32[4,32,128]{2,1,0:T(8,128)S(1)}, u32[]{:S(2)}, u32[]{:S(2)}) %collective-permute-start.8) | collective-permute-done | bytes 65568 | tf_op jit(solution)/shard_map/ppermute | solution.py:440
  27.8 1.8 %collective-permute-start.11 = (f32[32,128]{1,0:T(8,128)S(1)}, f32[32,128]{1,0:T(8,128)S(1)}, u32[]{:S(2)}, u32[]{:S(2)}) collective-permute-start(f32[32,128]{1,0:T(8,128)S(1)} %get-tuple-element.36), channel_id=1, source_target_pairs={{0,7},{1,6},{2,5},{3,4},{4,3},{5,2},{6,1},{7,0},{8,15},{9,14},{10,... | collective-permute-start | bytes 49160 | tf_op jit(solution)/shard_map/ppermute | solution.py:440
  29.6 0.0 collective-permute-start.10
  29.7 2.1 %collective-permute-start.9 = (f32[32,128]{1,0:T(8,128)S(1)}, f32[32,128]{1,0:T(8,128)S(1)}, u32[]{:S(2)}, u32[]{:S(2)}) collective-permute-start(f32[32,128]{1,0:T(8,128)S(1)} %get-tuple-element.35), channel_id=1, source_target_pairs={{0,3},{1,2},{2,1},{3,0},{4,7},{5,6},{6,5},{7,4},{8,11},{9,10},{10,... | collective-permute-start | bytes 49160 | tf_op jit(solution)/shard_map/ppermute | solution.py:440
  31.8 0.2 rest.1
  31.9 0.9 %collective-permute-done.11 = f32[32,128]{1,0:T(8,128)S(1)} collective-permute-done((f32[32,128]{1,0:T(8,128)S(1)}, f32[32,128]{1,0:T(8,128)S(1)}, u32[]{:S(2)}, u32[]{:S(2)}) %collective-permute-start.11) | collective-permute-done | bytes 16416 | tf_op jit(solution)/shard_map/ppermute | solution.py:440
  32.9 0.9 %collective-permute-done.10 = f32[32,128]{1,0:T(8,128)S(1)} collective-permute-done((f32[32,128]{1,0:T(8,128)S(1)}, f32[32,128]{1,0:T(8,128)S(1)}, u32[]{:S(2)}, u32[]{:S(2)}) %collective-permute-start.10) | collective-permute-done | bytes 16416 | tf_op jit(solution)/shard_map/ppermute | solution.py:440
  33.7 0.0 collective-permute-done.9
  33.7 1.6 %collective-permute-start.12 = (f32[32,128]{1,0:T(8,128)S(1)}, f32[32,128]{1,0:T(8,128)S(1)}, u32[]{:S(2)}, u32[]{:S(2)}) collective-permute-start(f32[32,128]{1,0:T(8,128)S(1)} %get-tuple-element.33.refs_0_), channel_id=1, source_target_pairs={{0,8},{8,0},{16,24},{24,16},{1,9},{9,1},{17,25},{25,17},{2,10},{10... | collective-permute-start | bytes 49160 | tf_op jit(solution)/shard_map/ppermute | solution.py:440
  35.3 1.5 %collective-permute-start.13 = (f32[32,128]{1,0:T(8,128)S(1)}, f32[32,128]{1,0:T(8,128)S(1)}, u32[]{:S(2)}, u32[]{:S(2)}) collective-permute-start(f32[32,128]{1,0:T(8,128)S(1)} %get-tuple-element.33.refs_0_), channel_id=1, source_target_pairs={{0,16},{8,24},{16,0},{24,8},{1,17},{9,25},{17,1},{25,9},{2,18},{10... | collective-permute-start | bytes 49160 | tf_op jit(solution)/shard_map/ppermute | solution.py:440
  36.8 0.5 %collective-permute-start.14 = (f32[32,128]{1,0:T(8,128)S(1)}, f32[32,128]{1,0:T(8,128)S(1)}, u32[]{:S(2)}, u32[]{:S(2)}) collective-permute-start(f32[32,128]{1,0:T(8,128)S(1)} %get-tuple-element.33.refs_0_), channel_id=1, source_target_pairs={{0,24},{8,16},{16,8},{24,0},{1,25},{9,17},{17,9},{25,1},{2,26},{10... | collective-permute-start | bytes 49160 | tf_op jit(solution)/shard_map/ppermute | solution.py:440
  37.3 0.7 %emit.1 = f32[1,2,32,64]{3,2,1,0:T(8,128)} custom-call(f32[32,128]{1,0:T(8,128)S(1)} %fusion.9.refs_0_), custom_call_target="tpu_custom_call" | custom-call | tf_op jit(solution)/shard_map/emit/pallas_call | solution.py:563
  38.0 0.0 collective-permute-done.12.refs_1_
  38.0 1.0 %collective-permute-done.13.refs_2_ = f32[32,128]{1,0:T(8,128)S(1)} collective-permute-done((f32[32,128]{1,0:T(8,128)S(1)}, f32[32,128]{1,0:T(8,128)S(1)}, u32[]{:S(2)}, u32[]{:S(2)}) %collective-permute-start.13) | collective-permute-done | bytes 16416 | tf_op jit(solution)/shard_map/ppermute | solution.py:440
  39.0 2.4 %collective-permute-done.14.refs_3_ = f32[32,128]{1,0:T(8,128)S(1)} collective-permute-done((f32[32,128]{1,0:T(8,128)S(1)}, f32[32,128]{1,0:T(8,128)S(1)}, u32[]{:S(2)}, u32[]{:S(2)}) %collective-permute-start.14) | collective-permute-done | bytes 16416 | tf_op jit(solution)/shard_map/ppermute | solution.py:440
  41.4 0.7 %fit.1 = (f32[1,2,32,64]{3,2,1,0:T(8,128)}, f32[1,2,32,64]{3,2,1,0:T(8,128)}) custom-call(f32[32,128]{1,0:T(8,128)S(1)} %get-tuple-element.33.refs_0_, f32[32,128]{1,0:T(8,128)S(1)} %collective-permute-done.12.refs_1_, f32[32,128]{1,0:T(8,128)S(1)} %collective-permute-done.13.refs_2_, f32[32,128]{1,0:T(8,128)S(1)} %collective-permute-done.14.refs_3_), custom_call_target="tpu_custom_call" | custom-call | tf_op jit(solution)/shard_map/fit/pallas_call | solution.py:572
  (5 shorter events, 0.0 us)
Async XLA Ops:
  1.6 6.5 %collective-permute-start.2 = (f32[72,128]{1,0:T(8,128)S(1)}, f32[72,128]{1,0:T(8,128)S(1)}, u32[]{:S(2)}, u32[]{:S(2)}) collective-permute-start(f32[72,128]{1,0:T(8,128)S(1)} %get-tuple-element.18), channel_id=1, source_target_pairs={{0,7},{1,6},{2,5},{3,4},{4,3},{5,2},{6,1},{7,0},{8,15},{9,14},{10,... | collective-permute-start | bytes 110600 | tf_op jit(solution)/shard_map/ppermute | solution.py:440
  6.2 4.6 %collective-permute-start.1 = (f32[72,128]{1,0:T(8,128)S(1)}, f32[72,128]{1,0:T(8,128)S(1)}, u32[]{:S(2)}, u32[]{:S(2)}) collective-permute-start(f32[72,128]{1,0:T(8,128)S(1)} %get-tuple-element.18), channel_id=1, source_target_pairs={{0,5},{1,4},{2,7},{3,6},{4,1},{5,0},{6,3},{7,2},{8,13},{9,12},{10,... | collective-permute-start | bytes 110600 | tf_op jit(solution)/shard_map/ppermute | solution.py:440
  6.2 4.6 %collective-permute-start = (f32[72,128]{1,0:T(8,128)S(1)}, f32[72,128]{1,0:T(8,128)S(1)}, u32[]{:S(2)}, u32[]{:S(2)}) collective-permute-start(f32[72,128]{1,0:T(8,128)S(1)} %get-tuple-element.18), channel_id=1, source_target_pairs={{0,3},{1,2},{2,1},{3,0},{4,7},{5,6},{6,5},{7,4},{8,11},{9,10},{10,... | collective-permute-start | bytes 110600 | tf_op jit(solution)/shard_map/ppermute | solution.py:440
  10.8 2.9 %collective-permute-start.3 = (f32[4,72,128]{2,1,0:T(8,128)S(1)}, f32[4,72,128]{2,1,0:T(8,128)S(1)}, u32[]{:S(2)}, u32[]{:S(2)}) collective-permute-start(f32[4,72,128]{2,1,0:T(8,128)S(1)} %pad_maximum_fusion.refs_2_.refs_1_.refs_0_), channel_id=1, source_target_pairs={{0,1},{1,0},{2,3},{3,2},{4,5},{5,4},{6,7},{7,6},{8,9},{9,8},{10,11... | collective-permute-start | bytes 442376 | tf_op jit(solution)/shard_map/ppermute | solution.py:440
  15.8 5.2 %collective-permute-start.6 = (f32[2,32,128]{2,1,0:T(8,128)S(1)}, f32[2,32,128]{2,1,0:T(8,128)S(1)}, u32[]{:S(2)}, u32[]{:S(2)}) collective-permute-start(f32[2,32,128]{2,1,0:T(8,128)S(1)} %first.1), channel_id=1, source_target_pairs={{0,7},{1,6},{2,5},{3,4},{4,3},{5,2},{6,1},{7,0},{8,15},{9,14},{10,... | collective-permute-start | bytes 98312 | tf_op jit(solution)/shard_map/ppermute | solution.py:440
  17.8 5.1 %collective-permute-start.5 = (f32[2,32,128]{2,1,0:T(8,128)S(1)}, f32[2,32,128]{2,1,0:T(8,128)S(1)}, u32[]{:S(2)}, u32[]{:S(2)}) collective-permute-start(f32[2,32,128]{2,1,0:T(8,128)S(1)} %first.1), channel_id=1, source_target_pairs={{0,5},{1,4},{2,7},{3,6},{4,1},{5,0},{6,3},{7,2},{8,13},{9,12},{10,... | collective-permute-start | bytes 98312 | tf_op jit(solution)/shard_map/ppermute | solution.py:440
  18.1 4.8 %collective-permute-start.4 = (f32[2,32,128]{2,1,0:T(8,128)S(1)}, f32[2,32,128]{2,1,0:T(8,128)S(1)}, u32[]{:S(2)}, u32[]{:S(2)}) collective-permute-start(f32[2,32,128]{2,1,0:T(8,128)S(1)} %first.1), channel_id=1, source_target_pairs={{0,3},{1,2},{2,1},{3,0},{4,7},{5,6},{6,5},{7,4},{8,11},{9,10},{10,... | collective-permute-start | bytes 98312 | tf_op jit(solution)/shard_map/ppermute | solution.py:440
  22.9 1.4 %collective-permute-start.7 = (f32[4,2,32,128]{3,2,1,0:T(8,128)S(1)}, f32[4,2,32,128]{3,2,1,0:T(8,128)S(1)}, u32[]{:S(2)}, u32[]{:S(2)}) collective-permute-start(f32[4,2,32,128]{3,2,1,0:T(8,128)S(1)} %pad_maximum_fusion.1.refs_3_), channel_id=1, source_target_pairs={{0,1},{1,0},{2,3},{3,2},{4,5},{5,4},{6,7},{7,6},{8,9},{9,8},{10,11... | collective-permute-start | bytes 393224 | tf_op jit(solution)/shard_map/ppermute | solution.py:440
  26.5 1.3 %collective-permute-start.8 = (f32[4,32,128]{2,1,0:T(8,128)S(1)}, f32[4,32,128]{2,1,0:T(8,128)S(1)}, u32[]{:S(2)}, u32[]{:S(2)}) collective-permute-start(f32[4,32,128]{2,1,0:T(8,128)S(1)} %get-tuple-element.30), channel_id=1, source_target_pairs={{0,1},{1,0},{2,3},{3,2},{4,5},{5,4},{6,7},{7,6},{8,9},{9,8},{10,11... | collective-permute-start | bytes 196616 | tf_op jit(solution)/shard_map/ppermute | solution.py:440
  27.8 5.0 %collective-permute-start.11 = (f32[32,128]{1,0:T(8,128)S(1)}, f32[32,128]{1,0:T(8,128)S(1)}, u32[]{:S(2)}, u32[]{:S(2)}) collective-permute-start(f32[32,128]{1,0:T(8,128)S(1)} %get-tuple-element.36), channel_id=1, source_target_pairs={{0,7},{1,6},{2,5},{3,4},{4,3},{5,2},{6,1},{7,0},{8,15},{9,14},{10,... | collective-permute-start | bytes 49160 | tf_op jit(solution)/shard_map/ppermute | solution.py:440
  29.6 4.1 %collective-permute-start.10 = (f32[32,128]{1,0:T(8,128)S(1)}, f32[32,128]{1,0:T(8,128)S(1)}, u32[]{:S(2)}, u32[]{:S(2)}) collective-permute-start(f32[32,128]{1,0:T(8,128)S(1)} %get-tuple-element.37), channel_id=1, source_target_pairs={{0,5},{1,4},{2,7},{3,6},{4,1},{5,0},{6,3},{7,2},{8,13},{9,12},{10,... | collective-permute-start | bytes 49160 | tf_op jit(solution)/shard_map/ppermute | solution.py:440
  29.7 4.1 %collective-permute-start.9 = (f32[32,128]{1,0:T(8,128)S(1)}, f32[32,128]{1,0:T(8,128)S(1)}, u32[]{:S(2)}, u32[]{:S(2)}) collective-permute-start(f32[32,128]{1,0:T(8,128)S(1)} %get-tuple-element.35), channel_id=1, source_target_pairs={{0,3},{1,2},{2,1},{3,0},{4,7},{5,6},{6,5},{7,4},{8,11},{9,10},{10,... | collective-permute-start | bytes 49160 | tf_op jit(solution)/shard_map/ppermute | solution.py:440
  33.7 4.3 %collective-permute-start.12 = (f32[32,128]{1,0:T(8,128)S(1)}, f32[32,128]{1,0:T(8,128)S(1)}, u32[]{:S(2)}, u32[]{:S(2)}) collective-permute-start(f32[32,128]{1,0:T(8,128)S(1)} %get-tuple-element.33.refs_0_), channel_id=1, source_target_pairs={{0,8},{8,0},{16,24},{24,16},{1,9},{9,1},{17,25},{25,17},{2,10},{10... | collective-permute-start | bytes 49160 | tf_op jit(solution)/shard_map/ppermute | solution.py:440
  35.3 3.7 %collective-permute-start.13 = (f32[32,128]{1,0:T(8,128)S(1)}, f32[32,128]{1,0:T(8,128)S(1)}, u32[]{:S(2)}, u32[]{:S(2)}) collective-permute-start(f32[32,128]{1,0:T(8,128)S(1)} %get-tuple-element.33.refs_0_), channel_id=1, source_target_pairs={{0,16},{8,24},{16,0},{24,8},{1,17},{9,25},{17,1},{25,9},{2,18},{10... | collective-permute-start | bytes 49160 | tf_op jit(solution)/shard_map/ppermute | solution.py:440
  36.8 4.6 %collective-permute-start.14 = (f32[32,128]{1,0:T(8,128)S(1)}, f32[32,128]{1,0:T(8,128)S(1)}, u32[]{:S(2)}, u32[]{:S(2)}) collective-permute-start(f32[32,128]{1,0:T(8,128)S(1)} %get-tuple-element.33.refs_0_), channel_id=1, source_target_pairs={{0,24},{8,16},{16,8},{24,0},{1,25},{9,17},{17,9},{25,1},{2,26},{10... | collective-permute-start | bytes 49160 | tf_op jit(solution)/shard_map/ppermute | solution.py:440
